TPU v7x, 128 devices: a whole 4x4x4 slice. The times are simulated.
128 devices in a mesh: sec: 8 (over z, core), blk: 16 (over y, x).
Axes of the slice: x: 4, y: 4, z: 4, core: 2. Of those that a mesh axis runs over, the one named last changes fastest.
Arguments:
- wavefunction: bfloat16 [8, 192, 128, 128], P('sec', 'blk')
- left_env: bfloat16 [8, 20, 192, 128, 128], P('sec', None, 'blk')
- right_env: bfloat16 [8, 20, 192, 128, 128], P('sec', None, 'blk')
- row_offset: int32 [8, 12], P('sec'), may hold values from 0 to 15, as said below
- sector_dims: int32 [8, 192, 2], P('sec', 'blk'), may hold values from 64 to 128
- trunc_ranks: int32 [8, 192], P('sec', 'blk'), may hold values from 32 to 128
Outputs:
- state_new: bfloat16 [8, 192, 128, 128], P('sec', 'blk')
- hstate_new: bfloat16 [8, 192, 128, 128], P('sec', 'blk')
- energy: float32 [8], P('sec')
- next_left: bfloat16 [8, 20, 192, 128, 128], P('sec', None, 'blk')
Inputs may be any that keep to these rules, and one draw needn't show every extreme that they name: The sector with up-charge u and down-charge e is stored in slot u of device (e + row_offset[u]) mod 16; in every section the offsets of some two adjacent up-charges differ by 16 / 2 modulo 16.
All inputs are finite; a program needn't handle non-finite values.
Results may differ from a plain program's by a relative error of at most 0.0067.
Values may be sent and summed in bfloat16 or wider, within the bound.
A program may use at most 128 MiB of HBM per device.

v0:
```python
import jax
import jax.numpy as jnp
from jax import lax
from jax.sharding import PartitionSpec as P


def passed_along(value, axis, by):
    length = lax.axis_size(axis)
    pairs = [(i, i + by) for i in range(length) if 0 <= i + by < length]
    return lax.ppermute(value, axis, pairs)


def route_blocks(state, offsets, device, nblk):
    count = state.shape[0]
    up_val = jnp.arange(count, dtype=jnp.int32)
    prev_off = jnp.roll(offsets, 1)
    next_off = jnp.roll(offsets, -1)
    down_val = (device - offsets) % nblk
    exists = [up_val >= 1, up_val <= count - 2, down_val >= 1, down_val <= nblk - 2]
    whole = lax.all_gather(state, "blk", axis=0, tiled=True)
    row_lo = jnp.clip(up_val - 1, 0, count - 1)
    row_hi = jnp.clip(up_val + 1, 0, count - 1)
    indices = [
        (down_val + prev_off) % nblk * count + row_lo,
        (down_val + next_off) % nblk * count + row_hi,
        (device - 1) % nblk * count + up_val,
        (device + 1) % nblk * count + up_val,
    ]
    picked = [jnp.take(whole, entry, axis=0) for entry in indices]
    result = [state]
    for ctype in range(4):
        result.append(
            jnp.where(exists[ctype][:, None, None], picked[ctype], jnp.zeros_like(picked[ctype]))
        )
    return result


def apply_ham(state, lenv, renv, mask, offsets, device, nblk):
    blocks = route_blocks(state, offsets, device, nblk)
    total = jnp.zeros(state.shape, jnp.float32)
    for ctype in range(5):
        inner = jnp.einsum(
            "wtab,tbc->wtac", lenv[ctype::5], blocks[ctype], preferred_element_type=jnp.float32
        ).astype(jnp.bfloat16)
        total = total + jnp.einsum(
            "wtac,wtdc->tad", inner, renv[ctype::5], preferred_element_type=jnp.float32
        )
    return total * mask


def shards(wavefunction, left_env, right_env, row_offset, sector_dims, trunc_ranks):
    start = wavefunction[0]
    lenv = left_env[0]
    renv = right_env[0]
    offsets = row_offset[0]
    dims = sector_dims[0]
    kept_cols = trunc_ranks[0]
    count = start.shape[0]
    width = start.shape[1]
    channels = lenv.shape[0]
    nblk = lax.axis_size("blk")
    device = lax.axis_index("blk")
    cells = float(count * nblk * width * width)
    lines = jnp.arange(width, dtype=jnp.int32)
    mask_on = (lines[None, :, None] < dims[:, 0][:, None, None]) & (
        lines[None, None, :] < dims[:, 1][:, None, None]
    )
    mask = mask_on.astype(jnp.float32)
    vzero = jnp.where(mask_on, start, jnp.zeros_like(start))
    hzero = apply_ham(vzero, lenv, renv, mask, offsets, device, nblk)
    vzero_f = vzero.astype(jnp.float32)
    nzero_part = jnp.sum(vzero_f * vzero_f)
    pzero_part = jnp.sum(vzero_f * hzero)
    nzero, pzero = lax.psum((nzero_part, pzero_part), "blk")
    scale = jnp.sqrt(cells / nzero)
    uzero = vzero_f * scale
    huzero = hzero * scale
    a_zero = pzero / nzero
    resid = huzero - a_zero * uzero
    squares = lax.psum(jnp.sum(resid * resid), "blk") / cells
    beta = jnp.sqrt(squares + 1e-06)
    vone = (resid / beta).astype(jnp.bfloat16)
    hone = apply_ham(vone, lenv, renv, mask, offsets, device, nblk)
    a_one = lax.psum(jnp.sum(vone.astype(jnp.float32) * hone), "blk") / cells
    half_gap = (a_zero - a_one) / 2.0
    ritz = (a_zero + a_one) / 2.0 - jnp.sqrt(half_gap * half_gap + beta * beta)
    gap_val = ritz - a_zero
    length = jnp.sqrt(beta * beta + gap_val * gap_val)
    xcoef = beta / length
    ycoef = gap_val / length
    state_new = (xcoef * uzero + ycoef * vone.astype(jnp.float32)).astype(jnp.bfloat16)
    hstate_new = (xcoef * huzero + ycoef * hone).astype(jnp.bfloat16)
    kept_on = lines[None, None, :] < kept_cols[:, None, None]
    kept = jnp.where(kept_on, state_new, jnp.zeros_like(state_new))
    kept_src = route_blocks(kept, offsets, device, nblk)
    pieces = []
    for ctype in range(5):
        inner = jnp.einsum(
            "wtab,tbc->wtac", lenv[ctype::5], kept_src[ctype], preferred_element_type=jnp.float32
        ).astype(jnp.bfloat16)
        piece = jnp.einsum(
            "tba,wtbc->wtac", kept, inner, preferred_element_type=jnp.float32
        ).astype(jnp.bfloat16)
        pieces.append(piece)
    stacked = jnp.stack(pieces, axis=1).reshape((channels, count, width, width))
    received = passed_along(stacked, "sec", 1)
    first_section = lax.axis_index("sec") == 0
    next_left = jnp.where(first_section, lenv, received)
    return (state_new[None], hstate_new[None], jnp.reshape(ritz, (1,)), next_left[None])


def solution(mesh):
    placed = (
        P("sec", "blk", None, None),
        P("sec", None, "blk", None, None),
        P("sec", None, "blk", None, None),
        P("sec", None),
        P("sec", "blk", None),
        P("sec", "blk"),
    )
    return jax.shard_map(
        shards,
        mesh=mesh,
        in_specs=placed,
        out_specs=(
            P("sec", "blk", None, None),
            P("sec", "blk", None, None),
            P("sec"),
            P("sec", None, "blk", None, None),
        ),
        check_vma=False,
    )
```

profile of v0, /device:TPU:64, one launch (start us, length us, event | category | flops | bytes accessed | tf_op | source)
XLA Modules:
  0.0 536.9 jit_solution(6096695522838150606)
XLA Ops:
  8.0 2.0 and_select_fusion
  10.3 1.3 fusion.370
  13.0 1.4 compare_and_fusion.2
  14.5 11.6 %copy_bitcast_fusion = (bf16[20,12,128,128]{3,2,0,1:T(8,128)(2,1)}, bf16[20,12,128,128]{3,2,0,1:T(8,128)(2,1)}) fusion(bf16[1,20,12,128,128]{4,3,2,1,0:T(8,128)(2,1)} %param.10, bf16[1,20,12,128,128]{4,3,2,1,0:T(8,128)(2,1)} %param.9), kind=kLoop, calls=%fused_computation.12 | loop fusion | bytes 31457280 | tf_op jit(solution)/shard_map/squeeze | solution.py:54
  26.0 2.9 fusion.45
  29.0 44.5 %all-gather.4.cloned.1.call-done = bf16[192,128,128]{2,1,0:T(8,128)(2,1)} async-done(((bf16[12,128,128]{2,1,0:T(8,128)(2,1)}), bf16[192,128,128]{2,1,0:T(8,128)(2,1)}) %all-gather.4.cloned.1.call-update) | async-done | bytes 6291472 | tf_op jit(solution)/shard_map/all_gather | solution.py:20
  73.5 3.4 gather_fusion
  76.9 3.4 fusion.140
  80.3 3.4 gather_fusion.1
  83.7 4.3 fusion.135
  88.0 3.4 gather_fusion.2
  91.5 3.6 fusion.130
  95.1 3.4 gather_fusion.3
  98.5 3.9 fusion.181
  102.4 39.1 %all-reduce = (f32[]{:T(128)}, f32[]{:T(128)}) all-reduce(f32[]{:T(128)} %get-tuple-element.10, f32[]{:T(128)} %get-tuple-element.9), channel_id=1, replica_groups=mesh['sec'=8,'blk'=16] {'blk'}, use_global_device_ids=true, to_apply=%region_3.5 | all-reduce | flops 2 | bytes 16 | tf_op jit(solution)/shard_map/psum | solution.py:74
  143.6 0.9 multiply_reduce_fusion
  144.5 36.1 %psum.30 = f32[]{:T(128)} all-reduce(f32[]{:T(128)} %multiply_reduce_fusion), channel_id=1, replica_groups=mesh['sec'=8,'blk'=16] {'blk'}, use_global_device_ids=true, to_apply=%region_5.7 | all-reduce | flops 1 | bytes 8 | tf_op jit(solution)/shard_map/psum | solution.py:80
  181.3 1.1 divide_convert_fusion
  182.7 3.0 fusion.70
  185.7 55.8 %all-gather.6.cloned.1.call-done = bf16[192,128,128]{2,1,0:T(8,128)(2,1)} async-done(((bf16[12,128,128]{2,1,0:T(8,128)(2,1)}), bf16[192,128,128]{2,1,0:T(8,128)(2,1)}) %all-gather.6.cloned.1.call-update) | async-done | bytes 6291472 | tf_op jit(solution)/shard_map/all_gather | solution.py:20
  241.5 3.4 gather_fusion.4
  244.9 4.3 fusion.115
  249.2 3.4 gather_fusion.5
  252.7 3.6 fusion.110
  256.3 3.4 gather_fusion.6
  259.7 4.3 fusion.105
  264.0 3.4 gather_fusion.7
  267.4 4.1 fusion.180
  271.5 39.3 %psum.31 = f32[]{:T(128)} all-reduce(f32[]{:T(128)} %get-tuple-element.29), channel_id=1, replica_groups=mesh['sec'=8,'blk'=16] {'blk'}, use_global_device_ids=true, to_apply=%region_7.9 | all-reduce | flops 1 | bytes 8 | tf_op jit(solution)/shard_map/psum | solution.py:84
  311.6 1.1 broadcast_select_fusion
  312.7 3.8 bitcast_dynamic-update-slice_fusion.4
  316.5 53.9 %all-gather.8.cloned.1.call-done = bf16[192,128,128]{2,1,0:T(8,128)(2,1)} async-done(((bf16[12,128,128]{2,1,0:T(8,128)(2,1)}), bf16[192,128,128]{2,1,0:T(8,128)(2,1)}) %all-gather.8.cloned.1.call-update) | async-done | bytes 6291472 | tf_op jit(solution)/shard_map/all_gather | solution.py:20
  370.4 3.4 gather_fusion.8
  373.8 4.0 bitcast_dynamic-update-slice_fusion.3
  377.8 3.4 gather_fusion.9
  381.2 3.9 bitcast_dynamic-update-slice_fusion.2
  385.2 3.4 gather_fusion.10
  388.6 3.9 bitcast_dynamic-update-slice_fusion.1
  392.5 3.4 gather_fusion.11
  395.9 3.9 bitcast_dynamic-update-slice_fusion
  399.8 10.7 %copy.40 = bf16[4,5,12,128,128]{4,3,2,1,0:T(8,128)(2,1)} copy(bf16[4,5,12,128,128]{3,4,0,2,1:T(8,128)(2,1)} %bitcast_dynamic-update-slice_fusion) | data formatting | bytes 15728640 | tf_op jit(solution)/shard_map/stack | solution.py:105
  410.5 9.9 %copy.41 = bf16[20,12,128,128]{3,2,0,1:T(8,128)(2,1)} copy(bf16[20,12,128,128]{3,2,1,0:T(8,128)(2,1)} %bitcast.313) | data formatting | bytes 15728640 | tf_op jit(solution)/shard_map/reshape | solution.py:105
  420.4 1.9 collective-permute-start
  422.3 1.1 fusion.314
  423.4 0.9 fusion.183
  424.3 85.6 %collective-permute-done = bf16[20,12,128,128]{3,2,0,1:T(8,128)(2,1)} collective-permute-done((bf16[20,12,128,128]{3,2,0,1:T(8,128)(2,1)}, bf16[20,12,128,128]{3,2,0,1:T(8,128)(2,1)}, u32[]{:S(2)}, u32[]{:S(2)}) %collective-permute-start) | collective-permute-done | bytes 7864352 | tf_op jit(solution)/shard_map/ppermute | solution.py:10
  509.9 9.4 %select_bitcast_fusion = bf16[1,20,12,128,128]{4,3,1,2,0:T(8,128)(2,1)} fusion(bf16[20,12,128,128]{3,2,0,1:T(8,128)(2,1)} %collective-permute-done, pred[]{:T(512)S(6)} %eq.20, bf16[1,20,12,128,128]{4,3,2,1,0:T(8,128)(2,1)} %param.9), kind=kLoop, calls=%fused_computation.14 | loop fusion | flops 3932160 | bytes 23592960 | tf_op jit(solution)/shard_map/broadcast_in_dim | solution.py:109
  519.3 9.9 %copy.42 = bf16[1,20,12,128,128]{4,3,2,1,0:T(8,128)(2,1)} copy(bf16[1,20,12,128,128]{4,3,1,2,0:T(8,128)(2,1)} %select_bitcast_fusion) | data formatting | bytes 15728640
  (29 shorter events, 2.8 us)
Async XLA Ops:
  7.2 66.3 %all-gather.4.cloned.1.call-start = ((), (), s32[]{:S(2)}) async-start(), calls=%async_computation | async-start | bytes 6684672 | tf_op jit(solution)/shard_map/all_gather | solution.py:20
  10.1 231.4 %all-gather.6.cloned.1.call-start = ((), (), s32[]{:S(2)}) async-start(), calls=%async_computation.1 | async-start | bytes 6684672 | tf_op jit(solution)/shard_map/all_gather | solution.py:20
  14.4 11.6 %copy-start.2 = (bf16[12,128,128]{2,1,0:T(8,128)(2,1)S(1)}, bf16[12,128,128]{2,1,0:T(8,128)(2,1)}, u32[]{:S(2)}) copy-start(bf16[12,128,128]{2,1,0:T(8,128)(2,1)} %and_select_fusion) | copy-start | bytes 1179652
  91.4 52.1 %copy-start = (bf16[1,12,128,128]{3,2,1,0:T(8,128)(2,1)S(1)}, bf16[1,12,128,128]{3,2,1,0:T(8,128)(2,1)}, u32[]{:S(2)}) copy-start(bf16[1,12,128,128]{3,2,1,0:T(8,128)(2,1)} %param.8) | copy-start | bytes 1179652
  95.1 87.5 %copy-start.4 = (s32[1,12]{1,0:T(1,128)S(1)}, s32[1,12]{1,0:T(1,128)}, u32[]{:S(2)}) copy-start(s32[1,12]{1,0:T(1,128)} %param.13) | copy-start | bytes 148
  182.4 188.0 %all-gather.8.cloned.1.call-start = ((), (), s32[]{:S(2)}) async-start(), calls=%async_computation.2 | async-start | bytes 6684672 | tf_op jit(solution)/shard_map/all_gather | solution.py:20
  252.6 14.8 %copy-start.1 = (bf16[12,128,128]{2,1,0:T(8,128)(2,1)S(1)}, bf16[12,128,128]{2,1,0:T(8,128)(2,1)}, u32[]{:S(2)}) copy-start(bf16[12,128,128]{2,1,0:T(8,128)(2,1)} %divide_convert_fusion) | copy-start | bytes 1179652
  312.7 68.5 %copy-start.3 = (bf16[12,128,128]{2,1,0:T(8,128)(2,1)S(1)}, bf16[12,128,128]{2,1,0:T(8,128)(2,1)}, u32[]{:S(2)}) copy-start(bf16[12,128,128]{2,1,0:T(8,128)(2,1)} %broadcast_select_fusion) | copy-start | bytes 1179652
  420.4 89.5 %collective-permute-start = (bf16[20,12,128,128]{3,2,0,1:T(8,128)(2,1)}, bf16[20,12,128,128]{3,2,0,1:T(8,128)(2,1)}, u32[]{:S(2)}, u32[]{:S(2)}) collective-permute-start(bf16[20,12,128,128]{3,2,0,1:T(8,128)(2,1)} %copy.41), channel_id=1, source_target_pairs={{0,16},{16,32},{32,48},{48,64},{64,80},{80,96},{96,112},{1,17},{17... | collective-permute-start | bytes 23592968 | tf_op jit(solution)/shard_map/ppermute | solution.py:10
Sparse Core Ops, SparseCore 0:
  10.7 62.7 all-gather.3
  182.5 58.9 all-gather.5
  312.8 57.5 all-gather.7
where the time goes:
time: 539 us; the launch traced here: 537 us
  waiting for transfers between devices  240 us (45%)
  blocking collectives  114 us (21%)
  local copies, waits for them, and re-layouts  85.8 us (16%)
  matrix products  57 us (11%)
  other arithmetic  18.8 us (3%)
  between operations  18.8 us (3%)
    all_gather x3, waiting for transfers between devices, route_blocks(): whole = lax.all_gather(state, 'blk', axis=0, tiled=True)  154 us
    ppermute x1, waiting for transfers between devices, passed_along(): return lax.ppermute(value, axis, pairs)  85.6 us
    gather x12, local copies, waits for them, and re-layouts, route_blocks(): picked = [jnp.take(whole, entry, axis=0) for entry in indices]  40.9 us
    psum x1, blocking collectives, shards(): a_one = lax.psum(jnp.sum(vone.astype(jnp.float32) * hone), 'blk') / cells  39.3 us
    psum x1, blocking collectives, shards(): nzero, pzero = lax.psum((nzero_part, pzero_part), 'blk')  39.1 us
    dot_general x10, matrix products, apply_ham(): jnp.einsum('wtac,wtdc->tad', inner, renv[ctype::5], preferred_element_typ...  37.5 us
    psum x1, blocking collectives, shards(): squares = lax.psum(jnp.sum(resid * resid), 'blk') / cells  36.1 us
    dot_general x5, matrix products, shards(): jnp.einsum('tba,wtbc->wtac', kept, inner, preferred_element_type=jnp.floa...  19.6 us
  transfers between devices with their start and end apart: 4, of which 4 were waited for; matrix products, arithmetic and copies ran while one was open for 5% of the time, Pallas kernels for 0%

commit v1 on v0

v1 whole, which is shorter than its diff:
```python
import functools

import jax
import jax.numpy as jnp
from jax import lax
from jax.experimental import pallas as pl
from jax.experimental.pallas import tpu as pltpu
from jax.sharding import PartitionSpec as P

MESH = pl.DeviceIdType.MESH
VMEM_SPEC = pl.BlockSpec(memory_space=pltpu.VMEM)
SMEM_SPEC = pl.BlockSpec(memory_space=pltpu.SMEM)
ANY_SPEC = pl.BlockSpec(memory_space=pl.ANY)
F32 = jnp.float32
BF16 = jnp.bfloat16
NB = 16
NU = 12
NC = 20
SB = 128
HALF = NU // 2
ROWS = 16
NCH = SB // ROWS


def lane_tile(values):
    row = lax.broadcasted_iota(jnp.int32, (8, SB), 0)
    lane = lax.broadcasted_iota(jnp.int32, (8, SB), 1)
    tile = jnp.zeros((8, SB), F32)
    for i, entries in enumerate(values):
        for u, entry in enumerate(entries):
            tile = jnp.where((row == i) & (lane == u), entry, tile)
    return tile


def slot_mask(dim_a, dim_b):
    line_a = lax.broadcasted_iota(jnp.int32, (SB, SB), 0)
    line_b = lax.broadcasted_iota(jnp.int32, (SB, SB), 1)
    return (line_a < dim_a) & (line_b < dim_b)


def exchange_kernel(first, off_ref, *refs):
    if first:
        dims_ref, trunc_ref, x_ref, v0_ref, o12_ref, o3_ref, o4_ref, os_ref, xs, small = refs[:10]
        rest = refs[10:]
    else:
        xs, small, o12_ref, o3_ref, o4_ref, os_ref = refs[:6]
        rest = refs[6:]
    recv1, sendb, side_s, side_r, s1s, s1r, s2s, s2r, sms, smr, loc = rest
    me = lax.axis_index("blk")
    par = me // NCH
    lo = pl.multiple_of((me % NCH) * ROWS, ROWS)

    barrier = pltpu.get_barrier_semaphore()
    for k in range(1, NB):
        pl.semaphore_signal(barrier, inc=1, device_id={"blk": (me + k) % NB}, device_id_type=MESH)

    if first:
        for u in range(NU):
            on = slot_mask(dims_ref[0, u, 0], dims_ref[0, u, 1])
            xs[u // 2, u % 2] = jnp.where(on, x_ref[u // 2, u % 2], jnp.zeros((SB, SB), BF16))
        small[...] = lane_tile([[trunc_ref[0, u].astype(F32) for u in range(NU)]])
    pl.semaphore_wait(barrier, NB - 1)

    def phase1(k):
        to = (me + k) % NB
        at = pl.multiple_of((to % NCH) * ROWS, ROWS)
        return pltpu.make_async_remote_copy(
            src_ref=xs.at[:, to // NCH, pl.ds(at, ROWS), :],
            dst_ref=recv1.at[me],
            send_sem=s1s.at[k],
            recv_sem=s1r.at[k],
            device_id={"blk": to},
            device_id_type=MESH,
        )

    def tiny(k):
        to = (me + k) % NB
        return pltpu.make_async_remote_copy(
            src_ref=small,
            dst_ref=os_ref.at[me],
            send_sem=sms.at[k],
            recv_sem=smr.at[k],
            device_id={"blk": to},
            device_id_type=MESH,
        )

    def side(i):
        return pltpu.make_async_remote_copy(
            src_ref=xs,
            dst_ref=(o3_ref, o4_ref)[i],
            send_sem=side_s.at[i],
            recv_sem=side_r.at[i],
            device_id={"blk": (me + (1, NB - 1)[i]) % NB},
            device_id_type=MESH,
        )

    def phase2(k):
        to = (me + k) % NB
        return pltpu.make_async_remote_copy(
            src_ref=sendb.at[to],
            dst_ref=o12_ref.at[:, pl.ds(par, HALF), 1 - par, pl.ds(lo, ROWS), :],
            send_sem=s2s.at[k],
            recv_sem=s2r.at[k],
            device_id={"blk": to},
            device_id_type=MESH,
        )

    @pl.loop(1, NB)
    def _(k):
        phase1(k).start()

    own1 = pltpu.make_async_copy(xs.at[:, par, pl.ds(lo, ROWS), :], recv1.at[me], loc.at[0])
    own1.start()
    own_small = pltpu.make_async_copy(small, os_ref.at[me], loc.at[1])
    own_small.start()
    copies = []
    if first:
        copies.append(pltpu.make_async_copy(xs, v0_ref, loc.at[3]))
        copies[0].start()
    side(0).start()
    side(1).start()

    @pl.loop(1, NB)
    def _(k):
        tiny(k).start()

    own1.wait()

    @pl.loop(1, NB)
    def _(k):
        phase1(k).wait_recv()

    @pl.loop(0, NB)
    def _(t):
        for r in range(HALF):
            up = 2 * r + par
            own = off_ref[0, up] + t + NB
            above = (own - off_ref[0, jnp.minimum(up + 1, NU - 1)]) & (NB - 1)
            below = (own - off_ref[0, jnp.maximum(up - 1, 0)]) & (NB - 1)
            sendb[t, 0, r] = recv1[above, r]
            sendb[t, 1, r] = recv1[below, r]

    @pl.loop(1, NB)
    def _(k):
        phase2(k).start()

    own2 = pltpu.make_async_copy(
        sendb.at[me], o12_ref.at[:, pl.ds(par, HALF), 1 - par, pl.ds(lo, ROWS), :], loc.at[2]
    )
    own2.start()
    for i in range(2):
        side(i).wait()

    @pl.loop(1, NB)
    def _(k):
        phase1(k).wait_send()
        tiny(k).wait()

    own2.wait()
    own_small.wait()
    for copy in copies:
        copy.wait()

    @pl.loop(1, NB)
    def _(k):
        phase2(k).wait()


def exchange(first, offsets, *args):
    pair = jax.ShapeDtypeStruct((HALF, 2, SB, SB), BF16)
    outs = [
        jax.ShapeDtypeStruct((2, HALF + 1, 2, SB, SB), BF16),
        pair,
        pair,
        jax.ShapeDtypeStruct((NB, 8, SB), F32),
    ]
    scratch = [
        pltpu.VMEM((NB, HALF, ROWS, SB), BF16),
        pltpu.VMEM((NB, 2, HALF, ROWS, SB), BF16),
        pltpu.SemaphoreType.DMA((2,)),
        pltpu.SemaphoreType.DMA((2,)),
    ] + [pltpu.SemaphoreType.DMA((NB,)) for _ in range(6)] + [pltpu.SemaphoreType.DMA((4,))]
    in_specs = [SMEM_SPEC, VMEM_SPEC, VMEM_SPEC]
    if first:
        in_specs = [SMEM_SPEC, SMEM_SPEC, SMEM_SPEC, VMEM_SPEC]
        outs = [pair] + outs
        scratch = [pltpu.VMEM((HALF, 2, SB, SB), BF16), pltpu.VMEM((8, SB), F32)] + scratch
    return pl.pallas_call(
        functools.partial(exchange_kernel, first),
        out_shape=outs,
        in_specs=in_specs,
        out_specs=[ANY_SPEC] * len(outs),
        scratch_shapes=scratch,
        compiler_params=pltpu.CompilerParams(collective_id=0 if first else 1, has_side_effects=True),
        name="exchange_v0" if first else "exchange_g",
    )(offsets, *args)


def hpsi(l_ref, r_ref, xs):
    inner = [None] * NC
    per = NC // 5
    for c in range(5):
        stack = jnp.concatenate([l_ref[c + 5 * k, 0] for k in range(per)], axis=0)
        product = jnp.dot(stack, xs[c], preferred_element_type=F32).astype(BF16)
        for k in range(per):
            inner[c + 5 * k] = product[k * SB : (k + 1) * SB]
    left = jnp.concatenate(inner, axis=1)
    right = jnp.concatenate([r_ref[w, 0] for w in range(NC)], axis=1)
    return lax.dot_general(left, right, (((1,), (1,)), ((), ())), preferred_element_type=F32)


def exists(off_ref, t, c):
    if c == 1:
        return t >= 1
    if c == 2:
        return t <= NU - 2
    down = (lax.axis_index("blk") + NB - off_ref[0, t]) & (NB - 1)
    return down >= 1 if c == 3 else down <= NB - 2


def source_device(off_ref, t, c):
    me = lax.axis_index("blk")
    if c == 1:
        return (me + NB - off_ref[0, t] + off_ref[0, jnp.maximum(t - 1, 0)]) & (NB - 1)
    if c == 2:
        return (me + NB - off_ref[0, t] + off_ref[0, jnp.minimum(t + 1, NU - 1)]) & (NB - 1)
    return (me + (NB - 1 if c == 3 else 1)) & (NB - 1)


def source_slot(t, c):
    if c == 1:
        return jnp.maximum(t - 1, 0)
    if c == 2:
        return jnp.minimum(t + 1, NU - 1)
    return t


def total(x):
    return jnp.sum(jnp.sum(x, axis=0, keepdims=True), axis=1, keepdims=True)


def put(tile_ref, row, t, value):
    rows = lax.broadcasted_iota(jnp.int32, (8, SB), 0)
    lanes = lax.broadcasted_iota(jnp.int32, (8, SB), 1)
    tile_ref[...] = jnp.where((rows == row) & (lanes == t), value, tile_ref[...])


def first_kernel(off_ref, dims_ref, l_ref, r_ref, v_ref, up_ref, dn_ref, e3_ref, e4_ref, h_ref, g_ref, s_ref):
    t = pl.program_id(0)
    zero = jnp.zeros((SB, SB), BF16)
    v = v_ref[0]
    xs = [v]
    for c, ref in ((1, up_ref), (2, dn_ref)):
        xs.append(jnp.where(exists(off_ref, t, c), ref[0, 0], zero))
    for c, ref in ((3, e3_ref), (4, e4_ref)):
        xs.append(jnp.where(exists(off_ref, t, c), ref[0], zero))
    h = jnp.where(slot_mask(dims_ref[0, t, 0], dims_ref[0, t, 1]), hpsi(l_ref, r_ref, xs), 0.0)
    vf = v.astype(F32)
    n = total(vf * vf)
    p = total(vf * h)
    alpha = jnp.where(n > 0.0, p / jnp.where(n > 0.0, n, 1.0), 0.0)
    g = h - alpha * vf
    h_ref[0] = h
    g_ref[0] = g.astype(BF16)

    @pl.when(t == 0)
    def _():
        s_ref[...] = jnp.zeros((8, SB), F32)

    put(s_ref, 0, t, n)
    put(s_ref, 1, t, p)
    put(s_ref, 2, t, total(g * g))
    put(s_ref, 3, t, alpha)


def slot_specs():
    env = pl.BlockSpec((NC, 1, SB, SB), lambda t, *_: (0, t, 0, 0))
    one = pl.BlockSpec((1, SB, SB), lambda t, *_: (t, 0, 0))
    up = pl.BlockSpec((1, 1, SB, SB), lambda t, *_: (0, jnp.maximum(t, 1), 0, 0))
    dn = pl.BlockSpec((1, 1, SB, SB), lambda t, *_: (1, jnp.minimum(t + 2, NU), 0, 0))
    tile = pl.BlockSpec((8, SB), lambda t, *_: (0, 0))
    tiles = pl.BlockSpec((NB, 8, SB), lambda t, *_: (0, 0, 0))
    return env, one, up, dn, tile, tiles


COST = pl.CostEstimate(flops=2 * 2 * NC * NU * SB**3, bytes_accessed=2 * 2 * NC * NU * SB**2, transcendentals=0)


def first_product(offsets, dims, lenv, renv, v, s12, s3, s4):
    env, one, up, dn, tile, _ = slot_specs()
    state = jax.ShapeDtypeStruct((NU, SB, SB), F32)
    return pl.pallas_call(
        first_kernel,
        grid_spec=pltpu.PrefetchScalarGridSpec(
            num_scalar_prefetch=2,
            grid=(NU,),
            in_specs=[env, env, one, up, dn, one, one],
            out_specs=[one, one, tile],
        ),
        out_shape=[state, jax.ShapeDtypeStruct((NU, SB, SB), BF16), jax.ShapeDtypeStruct((8, SB), F32)],
        cost_estimate=COST,
        name="first_product",
    )(offsets, dims, lenv, renv, v, s12, s12, s3, s4)


def second_kernel(
    off_ref, dims_ref, l_ref, r_ref, v_ref, up_ref, dn_ref, e3_ref, e4_ref, gup_ref, gdn_ref, g3_ref, g4_ref, h0_ref,
    sm_ref, sv_ref, v1_ref, src_ref, h_ref, q_ref, k_ref, acc
):
    t = pl.program_id(0)
    sums = sv_ref[...]
    nt, pt, rt, at = sums[:, 0, :], sums[:, 1, :], sums[:, 2, :], sums[:, 3, :]
    n = total(nt)
    a = total(pt) / n
    gap = at - a
    beta = jnp.sqrt(total(rt + gap * gap * nt) / n + 1e-6)
    scale = jnp.sqrt(float(NB * NU * SB * SB) / n)
    kappa = scale / beta
    v = v_ref[0].astype(F32)
    own = (kappa * (h0_ref[0] - a * v)).astype(BF16)
    xs = [own]
    sources = ((1, up_ref, gup_ref), (2, dn_ref, gdn_ref), (3, e3_ref, g3_ref), (4, e4_ref, g4_ref))
    for c, ref, gref in sources:
        lead = (0, 0) if c < 3 else (0,)
        alpha = sm_ref[source_device(off_ref, t, c), 3, source_slot(t, c)]
        x = kappa * (gref[lead].astype(F32) + (alpha - a) * ref[lead].astype(F32))
        x = jnp.where(exists(off_ref, t, c), x, 0.0).astype(BF16)
        src_ref[c - 1, 0] = x
        xs.append(x)
    h = jnp.where(slot_mask(dims_ref[0, t, 0], dims_ref[0, t, 1]), hpsi(l_ref, r_ref, xs), 0.0)
    v1_ref[0] = own
    h_ref[0] = h

    @pl.when(t == 0)
    def _():
        acc[...] = jnp.zeros((1, SB), F32)
        row = lax.broadcasted_iota(jnp.int32, (8, SB), 0)
        k_ref[...] = jnp.where(row == 0, a, jnp.where(row == 1, beta, scale))

    acc[...] += jnp.sum(own.astype(F32) * h, axis=0, keepdims=True)
    q_ref[...] = jnp.broadcast_to(acc[...], (8, SB))


def second_product(offsets, dims, lenv, renv, v, s12, s3, s4, g12, g3, g4, h0, sums):
    env, one, up, dn, tile, tiles = slot_specs()
    state = jax.ShapeDtypeStruct((NU, SB, SB), F32)
    return pl.pallas_call(
        second_kernel,
        grid_spec=pltpu.PrefetchScalarGridSpec(
            num_scalar_prefetch=2,
            grid=(NU,),
            in_specs=[env, env, one, up, dn, one, one, up, dn, one, one, one, SMEM_SPEC, tiles],
            out_specs=[one, pl.BlockSpec((4, 1, SB, SB), lambda t, *_: (0, t, 0, 0)), one, tile, tile],
            scratch_shapes=[pltpu.VMEM((1, SB), F32)],
        ),
        out_shape=[
            jax.ShapeDtypeStruct((NU, SB, SB), BF16),
            jax.ShapeDtypeStruct((4, NU, SB, SB), BF16),
            state,
            jax.ShapeDtypeStruct((8, SB), F32),
            jax.ShapeDtypeStruct((8, SB), F32),
        ],
        cost_estimate=COST,
        name="second_product",
    )(offsets, dims, lenv, renv, v, s12, s12, s3, s4, g12, g12, g3, g4, h0, sums, sums)


def kept_kernel(
    nsec, off_ref, tr_ref, q_ref, k_ref, v_ref, s12_ref, s3_ref, s4_ref, v1_ref, src_ref, kept_ref, coef_ref,
    kept, qs, q_send, q_recv, z_send, z_recv
):
    me = lax.axis_index("blk")
    sec = lax.axis_index("sec")
    after = {"sec": (sec + 1) % nsec}
    barrier = pltpu.get_barrier_semaphore()
    for k in range(1, NB):
        pl.semaphore_signal(barrier, inc=1, device_id={"blk": (me + k) % NB}, device_id_type=MESH)
    pl.semaphore_signal(barrier, inc=1, device_id=after, device_id_type=MESH)
    pl.semaphore_signal(barrier, inc=1, device_id={"sec": (sec + nsec - 1) % nsec}, device_id_type=MESH)
    pl.semaphore_wait(barrier, NB + 1)

    def tiny(k):
        return pltpu.make_async_remote_copy(
            src_ref=q_ref,
            dst_ref=qs.at[me],
            send_sem=q_send.at[k],
            recv_sem=q_recv.at[k],
            device_id={"blk": (me + k) % NB},
            device_id_type=MESH,
        )

    @pl.loop(1, NB)
    def _(k):
        tiny(k).start()

    qs[me] = q_ref[...]

    @pl.loop(1, NB)
    def _(k):
        tiny(k).wait()

    a0, beta, scale = k_ref[0:1, 0:1], k_ref[1:2, 0:1], k_ref[2:3, 0:1]
    a1 = total(jnp.sum(qs[...], axis=0)[0:1]) / float(NB * NU * SB * SB)
    half = (a0 - a1) / 2.0
    ritz = (a0 + a1) / 2.0 - jnp.sqrt(half * half + beta * beta)
    gap = ritz - a0
    length = jnp.sqrt(beta * beta + gap * gap)
    xcoef, ycoef = beta / length, gap / length
    row = lax.broadcasted_iota(jnp.int32, (8, SB), 0)
    coef_ref[...] = jnp.where(row == 0, ritz, jnp.where(row == 1, xcoef, jnp.where(row == 2, ycoef, scale)))
    lane = lax.broadcasted_iota(jnp.int32, (SB, SB), 1).astype(F32)

    def send(c):
        return pltpu.make_async_remote_copy(
            src_ref=kept.at[c],
            dst_ref=kept_ref.at[c],
            send_sem=z_send.at[c],
            recv_sem=z_recv.at[c],
            device_id=after,
            device_id_type=MESH,
        )

    for c in range(5):

        @pl.loop(0, NU)
        def _(t):
            if c == 0:
                v, v1 = v_ref[t], v1_ref[t]
                rank = tr_ref[me, 0, t]
            else:
                v1 = src_ref[c - 1, t]
                rank = tr_ref[source_device(off_ref, t, c), 0, source_slot(t, c)]
                if c == 1:
                    v = s12_ref[0, jnp.maximum(t, 1)]
                elif c == 2:
                    v = s12_ref[1, jnp.minimum(t + 2, NU)]
                else:
                    v = (s3_ref, s4_ref)[c - 3][t]
            x = xcoef * (v.astype(F32) * scale) + ycoef * v1.astype(F32)
            on = lane < rank
            if c:
                on = on & exists(off_ref, t, c)
            kept[c, t] = jnp.where(on, x, 0.0).astype(BF16)

    for c in range(5):
        send(c).start()
    for c in range(5):
        send(c).wait()


def kept_blocks(nsec, offsets, ranks, q, k, v, s12, s3, s4, v1, src):
    blocks = (5, NU, SB, SB)
    return pl.pallas_call(
        functools.partial(kept_kernel, nsec),
        out_shape=[jax.ShapeDtypeStruct(blocks, BF16), jax.ShapeDtypeStruct((8, SB), F32)],
        in_specs=[SMEM_SPEC, SMEM_SPEC] + [VMEM_SPEC] * 8,
        out_specs=[ANY_SPEC, VMEM_SPEC],
        scratch_shapes=[
            pltpu.VMEM(blocks, BF16),
            pltpu.VMEM((NB, 8, SB), F32),
            pltpu.SemaphoreType.DMA((NB,)),
            pltpu.SemaphoreType.DMA((NB,)),
            pltpu.SemaphoreType.DMA((5,)),
            pltpu.SemaphoreType.DMA((5,)),
        ],
        compiler_params=pltpu.CompilerParams(collective_id=2, has_side_effects=True),
        name="kept_blocks",
    )(offsets, ranks, q, k, v, s12, s3, s4, v1, src)


def update_kernel(head_ref, coef_ref, own_ref, l_ref, k_ref, v_ref, v1_ref, h0_ref, h1_ref, next_ref, s_ref, hs_ref):
    first_section = head_ref[0] == 1
    xcoef, ycoef, scale = coef_ref[1:2, 0:1], coef_ref[2:3, 0:1], coef_ref[3:4, 0:1]
    s_ref[0] = (xcoef * (v_ref[0].astype(F32) * scale) + ycoef * v1_ref[0].astype(F32)).astype(BF16)
    hs_ref[0] = (xcoef * (h0_ref[0] * scale) + ycoef * h1_ref[0]).astype(BF16)

    @pl.when(first_section)
    def _():
        next_ref[...] = own_ref[...]

    @pl.when(jnp.logical_not(first_section))
    def _():
        per = NC // 5
        kept = k_ref[0, 0]
        for c in range(5):
            stack = jnp.concatenate([l_ref[c + 5 * k, 0] for k in range(per)], axis=0)
            inner = jnp.dot(stack, k_ref[c, 0], preferred_element_type=F32).astype(BF16)
            wide = jnp.concatenate([inner[k * SB : (k + 1) * SB] for k in range(per)], axis=1)
            out = lax.dot_general(kept, wide, (((0,), (0,)), ((), ())), preferred_element_type=F32).astype(BF16)
            for k in range(per):
                next_ref[c + 5 * k, 0] = out[:, k * SB : (k + 1) * SB]


def update(head, coef, lenv, prev, kept, v, v1, h0, h1):
    _, one, _, _, tile, _ = slot_specs()
    own = pl.BlockSpec((NC, 1, SB, SB), lambda t, head: (0, t * head[0], 0, 0))
    far = pl.BlockSpec((NC, 1, SB, SB), lambda t, head: (0, t * (1 - head[0]), 0, 0))
    state = jax.ShapeDtypeStruct((NU, SB, SB), BF16)
    return pl.pallas_call(
        update_kernel,
        grid_spec=pltpu.PrefetchScalarGridSpec(
            num_scalar_prefetch=1,
            grid=(NU,),
            in_specs=[
                tile, own, far, pl.BlockSpec((5, 1, SB, SB), lambda t, *_: (0, t, 0, 0)), one, one, one, one,
            ],
            out_specs=[pl.BlockSpec((NC, 1, SB, SB), lambda t, *_: (0, t, 0, 0)), one, one],
        ),
        out_shape=[jax.ShapeDtypeStruct((NC, NU, SB, SB), BF16), state, state],
        cost_estimate=COST,
        name="update",
    )(head, coef, lenv, prev, kept, v, v1, h0, h1)


def shards(wavefunction, left_env, right_env, offsets, dims, ranks):
    nsec = lax.axis_size("sec")
    lenv, renv = left_env[0], right_env[0]
    pairs = (HALF, 2, SB, SB)
    flat = (NU, SB, SB)
    prev = lax.ppermute(lenv, "sec", [(i, i + 1) for i in range(nsec - 1)])
    v, s12, s3, s4, rank_all = exchange(True, offsets, dims, ranks, wavefunction[0].reshape(pairs))
    v, s3, s4 = v.reshape(flat), s3.reshape(flat), s4.reshape(flat)
    s12 = s12.reshape((2, NU + 2, SB, SB))
    h0, g, sums = first_product(offsets, dims, lenv, renv, v, s12, s3, s4)
    g12, g3, g4, sums_all = exchange(False, offsets, g.reshape(pairs), sums)
    g3, g4 = g3.reshape(flat), g4.reshape(flat)
    g12 = g12.reshape((2, NU + 2, SB, SB))
    v1, src, h1, q, k = second_product(offsets, dims, lenv, renv, v, s12, s3, s4, g12, g3, g4, h0, sums_all)
    kept, coef = kept_blocks(nsec, offsets, rank_all, q, k, v, s12, s3, s4, v1, src)
    head = jnp.where(lax.axis_index("sec") == 0, 1, 0).astype(jnp.int32).reshape((1,))
    next_left, state, hstate = update(head, coef, lenv, prev, kept, v, v1, h0, h1)
    return state[None], hstate[None], coef[0, 0:1], next_left[None]


def solution(mesh):
    placed = (
        P("sec", "blk", None, None),
        P("sec", None, "blk", None, None),
        P("sec", None, "blk", None, None),
        P("sec", None),
        P("sec", "blk", None),
        P("sec", "blk"),
    )
    return jax.shard_map(
        shards,
        mesh=mesh,
        in_specs=placed,
        out_specs=(
            P("sec", "blk", None, None),
            P("sec", "blk", None, None),
            P("sec"),
            P("sec", None, "blk", None, None),
        ),
        check_vma=False,
    )
```

time: 539 us -> 159 us (0.29)
  waiting for transfers between devices: 240 us -> 0.01 us
  Pallas kernels: 0 us -> 152 us
  blocking collectives: 114 us -> 0 us
  local copies, waits for them, and re-layouts: 85.8 us -> 2.54 us
  matrix products: 57 us -> 0 us
  other arithmetic: 18.8 us -> 0 us
  between operations: 18.8 us -> 0.68 us
    all_gather x3 -> x0, waiting for transfers between devices: 154 us -> none  [route_blocks(): whole = lax.all_gather(state, 'blk', axis=0, tiled=True)]
    pallas_call x0 -> x6, Pallas kernels: none -> 152 us  [the longest x2 66.9 us: exchange(): pl.pallas_call(functools.partial(exchange_kernel, first), out_shape=outs,...]
    psum x3 -> x0, blocking collectives: 114 us -> none  [the longest x1 39.3 us: shards(): a_one = lax.psum(jnp.sum(vone.astype(jnp.float32) * hone), 'blk') / cells]
    ppermute x1, waiting for transfers between devices: 85.6 us -> 0.01 us  [shards(): prev = lax.ppermute(lenv, 'sec', [(i, i + 1) for i in range(nsec - 1)])]
    dot_general x15 -> x0, matrix products: 57 us -> none  [the longest x10 37.5 us: apply_ham(): jnp.einsum('wtac,wtdc->tad', inner, renv[ctype::5], preferred_element_typ...]
    gather x12 -> x0, local copies, waits for them, and re-layouts: 40.9 us -> none  [route_blocks(): picked = [jnp.take(whole, entry, axis=0) for entry in indices]]
    squeeze x1 -> x0, local copies, waits for them, and re-layouts: 11.6 us -> none  [shards(): renv = right_env[0]]
    broadcast_in_dim x3 -> x0, other arithmetic: 11.4 us -> none  [the longest x1 9.42 us: shards(): next_left[None]]
  transfers between devices with their start and end apart: 4 -> 1, of which waited for: 4 -> 0; matrix products, arithmetic and copies ran while one was open for 5% -> 2% of each run, Pallas kernels for 0% -> 87%
where the time goes in v1:
time: 159 us; the launch traced here: 157 us
  Pallas kernels  152 us (96%)
  local copies, waits for them, and re-layouts  2.54 us (2%)
  starting transfers between devices  1.92 us (1%)
    pallas_call x2, Pallas kernels, exchange(): pl.pallas_call(functools.partial(exchange_kernel, first), out_shape=outs,...  66.9 us
    pallas_call x1, Pallas kernels, kept_blocks(): pl.pallas_call(functools.partial(kept_kernel, nsec), out_shape=[jax.Shape...  36.1 us
    pallas_call x1, Pallas kernels, second_product(): pl.pallas_call(second_kernel, grid_spec=pltpu.PrefetchScalarGridSpec(num_...  18.4 us
    pallas_call x1, Pallas kernels, first_product(): pl.pallas_call(first_kernel, grid_spec=pltpu.PrefetchScalarGridSpec(num_s...  16.4 us
    pallas_call x1, Pallas kernels, update(): pl.pallas_call(update_kernel, grid_spec=pltpu.PrefetchScalarGridSpec(num_...  14.6 us
  transfers between devices with their start and end apart: 1, of which 0 were waited for; matrix products, arithmetic and copies ran while one was open for 2% of the time, Pallas kernels for 87%

profile of v1, /device:TPU:64, one launch (start us, length us, event | category | flops | bytes accessed | tf_op | source)
XLA Modules:
  0.0 157.5 jit_solution(6759636858871112039)
XLA Ops:
  0.6 1.9 %collective-permute-start = (bf16[20,12,128,128]{3,2,1,0:T(8,128)(2,1)}, bf16[20,12,128,128]{3,2,1,0:T(8,128)(2,1)}, u32[]{:S(2)}, u32[]{:S(2)}) collective-permute-start(bf16[20,12,128,128]{3,2,1,0:T(8,128)(2,1)} %bitcast.16), channel_id=1, source_target_pairs={{0,16},{16,32},{32,48},{48,64},{64,80},{80,96},{96,112},{1,17},{17... | collective-permute-start | bytes 23592968 | tf_op jit(solution)/shard_map/ppermute | solution.py:520
  2.6 1.4 copy.10.refs_0_.dims_ref
  3.9 32.9 %exchange_v0.1 = (bf16[6,2,128,128]{3,2,1,0:T(8,128)(2,1)}, bf16[2,7,2,128,128]{4,3,2,1,0:T(8,128)(2,1)}, bf16[6,2,128,128]{3,2,1,0:T(8,128)(2,1)}, bf16[6,2,128,128]{3,2,1,0:T(8,128)(2,1)}, f32[16,8,128]{2,1,0:T(8,128)}) custom-call(s32[1,12]{1,0:T(1,128)} %off_ref.9, s32[1,12,2]{2,1,0:T(8,128)} %copy.10.refs_0_.dims_ref, s32[1,12]{1,0:T(1,128)} %refs_1_.1, ...), custom_call_target="tpu_custom_call" | custom-call | tf_op jit(solution)/shard_map/exchange_v0/pallas_call | solution.py:188
  36.8 16.4 %first_product.1 = (f32[12,128,128]{2,1,0:T(8,128)}, bf16[12,128,128]{2,1,0:T(8,128)(2,1)}, f32[8,128]{1,0:T(8,128)}) custom-call(s32[1,12]{1,0:T(1,128)} %off_ref.9, s32[1,12,2]{2,1,0:T(8,128)} %copy.10.refs_0_.dims_ref, bf16[20,12,128,128]{3,2,1,0:T(8,128)(2,1)} %bitcast.17, bf16[20,12,128,128]{3,2,1,0:T(8,128)(2,1)} %bitcast.20, ...), custom_call_target="tpu_custom_call" | custom-call | flops 2013265920 | bytes 15728640 | tf_op jit(solution)/shard_map/first_product/pallas_call | solution.py:292
  53.2 34.0 %exchange_g.1 = (bf16[2,7,2,128,128]{4,3,2,1,0:T(8,128)(2,1)}, bf16[6,2,128,128]{3,2,1,0:T(8,128)(2,1)}, bf16[6,2,128,128]{3,2,1,0:T(8,128)(2,1)}, f32[16,8,128]{2,1,0:T(8,128)}) custom-call(s32[1,12]{1,0:T(1,128)} %off_ref.9, bf16[6,2,128,128]{3,2,1,0:T(8,128)(2,1)} %bitcast.40, f32[8,128]{1,0:T(8,128)} %get-tuple-element.32.refs_1_), custom_call_target="tpu_custom_call" | custom-call | tf_op jit(solution)/shard_map/exchange_g/pallas_call | solution.py:188
  87.2 18.4 %second_product.1 = (bf16[12,128,128]{2,1,0:T(8,128)(2,1)}, bf16[4,12,128,128]{3,2,1,0:T(8,128)(2,1)}, f32[12,128,128]{2,1,0:T(8,128)}, f32[8,128]{1,0:T(8,128)}, f32[8,128]{1,0:T(8,128)}) custom-call(s32[1,12]{1,0:T(1,128)} %off_ref.9, s32[1,12,2]{2,1,0:T(8,128)} %copy.10.refs_0_.dims_ref, bf16[20,12,128,128]{3,2,1,0:T(8,128)(2,1)} %bitcast.18, ...), custom_call_target="tpu_custom_call" | custom-call | flops 2013265920 | bytes 15728640 | tf_op jit(solution)/shard_map/second_product/pallas_call | solution.py:347
  105.6 36.1 %kept_blocks.1 = (bf16[5,12,128,128]{3,2,1,0:T(8,128)(2,1)}, f32[8,128]{1,0:T(8,128)}) custom-call(s32[1,12]{1,0:T(1,128)} %off_ref.9, f32[16,8,128]{2,1,0:T(8,128)} %get-tuple-element.26.tr_ref, f32[8,128]{1,0:T(8,128)} %get-tuple-element.38.q_ref, f32[8,128]{1,0:T(8,128)} %get-tuple-element.39.k_ref, bf16[12,128,128]{2,1,0:T(8,128)(2,1)} %bitcast.29, ...), custom_call_target="tpu_custom_call" | custom-call | tf_op jit(solution)/shard_map/kept_blocks/pallas_call | solution.py:453
  141.7 1.2 slice.3
  142.9 0.0 collective-permute-done.l_ref
  142.9 14.6 %update.1 = (bf16[20,12,128,128]{3,2,1,0:T(8,128)(2,1)}, bf16[12,128,128]{2,1,0:T(8,128)(2,1)}, bf16[12,128,128]{2,1,0:T(8,128)(2,1)}) custom-call(s32[1]{0:T(128)} %bitcast.head_ref, f32[8,128]{1,0:T(8,128)} %get-tuple-element.42.coef_ref, bf16[20,12,128,128]{3,2,1,0:T(8,128)(2,1)} %bitcast.19, bf16[20,12,128,128]{3,2,1,0:T(8,128)(2,1)} %collective-permute-done.l_ref, ...), custom_call_target="tpu_custom_call" | custom-call | flops 2013265920 | bytes 15728640 | tf_op jit(solution)/shard_map/update/pallas_call | solution.py:499
Async XLA Ops:
  0.6 142.3 %collective-permute-start = (bf16[20,12,128,128]{3,2,1,0:T(8,128)(2,1)}, bf16[20,12,128,128]{3,2,1,0:T(8,128)(2,1)}, u32[]{:S(2)}, u32[]{:S(2)}) collective-permute-start(bf16[20,12,128,128]{3,2,1,0:T(8,128)(2,1)} %bitcast.16), channel_id=1, source_target_pairs={{0,16},{16,32},{32,48},{48,64},{64,80},{80,96},{96,112},{1,17},{17... | collective-permute-start | bytes 23592968 | tf_op jit(solution)/shard_map/ppermute | solution.py:520

commit v2 on v0

v2 whole, which is shorter than its diff:
```python
import functools

import jax
import jax.numpy as jnp
from jax import lax
from jax.experimental import pallas as pl
from jax.experimental.pallas import tpu as pltpu
from jax.sharding import PartitionSpec as P

MESH = pl.DeviceIdType.MESH
VMEM_SPEC = pl.BlockSpec(memory_space=pltpu.VMEM)
SMEM_SPEC = pl.BlockSpec(memory_space=pltpu.SMEM)
ANY_SPEC = pl.BlockSpec(memory_space=pl.ANY)
F32 = jnp.float32
BF16 = jnp.bfloat16
NB = 16
NU = 12
NC = 20
SB = 128
HALF = NU // 2
ROWS = 16
NCH = SB // ROWS
PER = NC // 5
FAR = 6
CELLS = float(NB * NU * SB * SB)


def lane_tile(values):
    row = lax.broadcasted_iota(jnp.int32, (8, SB), 0)
    lane = lax.broadcasted_iota(jnp.int32, (8, SB), 1)
    tile = jnp.zeros((8, SB), F32)
    for i, entries in enumerate(values):
        for u, entry in enumerate(entries):
            tile = jnp.where((row == i) & (lane == u), entry, tile)
    return tile


def slot_mask(dim_a, dim_b):
    line_a = lax.broadcasted_iota(jnp.int32, (SB, SB), 0)
    line_b = lax.broadcasted_iota(jnp.int32, (SB, SB), 1)
    return (line_a < dim_a) & (line_b < dim_b)


def exists(off_ref, t, c):
    if c == 1:
        return t >= 1
    if c == 2:
        return t <= NU - 2
    down = (lax.axis_index("blk") + NB - off_ref[0, t]) & (NB - 1)
    return down >= 1 if c == 3 else down <= NB - 2


def source_device(off_ref, t, c):
    me = lax.axis_index("blk")
    if c == 1:
        return (me + NB - off_ref[0, t] + off_ref[0, jnp.maximum(t - 1, 0)]) & (NB - 1)
    if c == 2:
        return (me + NB - off_ref[0, t] + off_ref[0, jnp.minimum(t + 1, NU - 1)]) & (NB - 1)
    return (me + (NB - 1 if c == 3 else 1)) & (NB - 1)


def source_slot(t, c):
    if c == 1:
        return jnp.maximum(t - 1, 0)
    if c == 2:
        return jnp.minimum(t + 1, NU - 1)
    return t


def total(x):
    return jnp.sum(jnp.sum(x, axis=0, keepdims=True), axis=1, keepdims=True)


def far_entry(tiles_ref, device, row, slot):
    lane = lax.broadcasted_iota(jnp.int32, (8, SB), 1)
    rows = lax.broadcasted_iota(jnp.int32, (8, SB), 0)
    return total(jnp.where((lane == slot) & (rows == row), tiles_ref[device], 0.0))


def products(l_ref, r_ref, acc_ref, work, fresh):
    inner = []
    for c, t, x in work:
        stack = jnp.concatenate([l_ref[c + 5 * k, t] for k in range(PER)], axis=0)
        product = jnp.dot(stack, x, preferred_element_type=F32).astype(BF16)
        inner.append(jnp.concatenate([product[k * SB : (k + 1) * SB] for k in range(PER)], axis=1))
    sums = {}
    slots = {}
    for left, (c, t, _) in zip(inner, work):
        right = jnp.concatenate([r_ref[c + 5 * k, t] for k in range(PER)], axis=1)
        term = lax.dot_general(left, right, (((1,), (1,)), ((), ())), preferred_element_type=F32)
        key = id(t)
        sums[key] = sums[key] + term if key in sums else term
        slots[key] = t
    for key, t in slots.items():
        acc_ref[t] = sums[key] if fresh else acc_ref[t] + sums[key]


def main_kernel(
    nsec, off_ref, dims_ref, rank_ref, x_ref, l_hbm, r_hbm,
    prev_ref, rel1, rel2, kept_ref, state_ref, hstate_ref, coef_ref,
    lv, rv, xs, va, v3, v4, gs, ga, g3, g4, recv_v, recv_g, send_v, send_g, h0, h1, v1, vs, kept, st, hst,
    ranks, ranks_all, sums, sums_all, qt, qt_all,
    l_sem, r_sem, side_s, side_r, p1s, p1r, p2s, p2r, ts, tr, loc, zs, zr, ks, kr, fin
):
    me = lax.axis_index("blk")
    sec = lax.axis_index("sec")
    odd = sec % 2 == 1
    par = me // NCH
    lo = pl.multiple_of((me % NCH) * ROWS, ROWS)

    def section(by):
        return {"sec": (sec + by + nsec) % nsec}

    def peer(k):
        return {"blk": (me + k) % NB}

    def remote(src, dst, send, recv, where):
        return pltpu.make_async_remote_copy(
            src_ref=src, dst_ref=dst, send_sem=send, recv_sem=recv, device_id=where, device_id_type=MESH
        )

    barrier = pltpu.get_barrier_semaphore()
    for k in range(1, NB):
        pl.semaphore_signal(barrier, inc=1, device_id=peer(k), device_id_type=MESH)
    for by in (1, -1, 2, -2, 3, -3):
        pl.semaphore_signal(barrier, inc=1, device_id=section(by), device_id_type=MESH)

    def load(w, i):
        src, dst, sem = ((l_hbm, lv, l_sem), (r_hbm, rv, r_sem))[i]
        return pltpu.make_async_copy(src.at[w], dst.at[w], sem.at[w])

    for c in (0, 3, 4, 1, 2):
        for k in range(PER):
            load(c + 5 * k, 0).start()
            load(c + 5 * k, 1).start()

    def loaded(c):
        for k in range(PER):
            load(c + 5 * k, 0).wait()
            load(c + 5 * k, 1).wait()

    for u in range(NU):
        on = slot_mask(dims_ref[0, 0, u], dims_ref[0, 1, u])
        xs[u // 2, u % 2] = jnp.where(on, x_ref[u // 2, u % 2], jnp.zeros((SB, SB), BF16))
    ranks[...] = lane_tile([[rank_ref[0, u].astype(F32) for u in range(NU)]])
    sums[...] = jnp.zeros((8, SB), F32)
    pl.semaphore_wait(barrier, NB + 5)

    state_of = (xs, gs)
    recv_of = (recv_v, recv_g)
    send_of = (send_v, send_g)
    wide_of = (va, ga)
    side_of = ((v3, v4), (g3, g4))
    tile_of = (ranks, sums, qt)
    tiles_of = (ranks_all, sums_all, qt_all)

    def phase1(i, k):
        to = (me + k) % NB
        at = pl.multiple_of((to % NCH) * ROWS, ROWS)
        return remote(
            state_of[i].at[:, to // NCH, pl.ds(at, ROWS), :], recv_of[i].at[me], p1s.at[i, k], p1r.at[i, k], peer(k)
        )

    def mine(ref):
        return ref.at[:, pl.ds(par, HALF), 1 - par, pl.ds(lo, ROWS), :]

    def phase2(i, k):
        return remote(send_of[i].at[(me + k) % NB], mine(wide_of[i]), p2s.at[i, k], p2r.at[i, k], peer(k))

    def side(i, j):
        return remote(state_of[i], side_of[i][j], side_s.at[i, j], side_r.at[i, j], peer((1, NB - 1)[j]))

    def tiny(i, k):
        return remote(tile_of[i], tiles_of[i].at[me], ts.at[i, k], tr.at[i, k], peer(k))

    def own1(i):
        return pltpu.make_async_copy(state_of[i].at[:, par, pl.ds(lo, ROWS), :], recv_of[i].at[me], loc.at[i, 0])

    def own2(i):
        return pltpu.make_async_copy(send_of[i].at[me], mine(wide_of[i]), loc.at[i, 1])

    def direct(channels):
        part = pl.ds(0, channels)
        return remote(l_hbm.at[part], prev_ref.at[part], zs.at[0], zr.at[0], section(1))

    far = pl.ds(NC - FAR, FAR)

    def hop(i):
        if i == 0:
            return remote(l_hbm.at[far], rel1, zs.at[1], zr.at[1], section(-2))
        if i == 1:
            return remote(rel1, rel2, zs.at[2], zr.at[2], section(-2))
        return remote(rel2, prev_ref.at[far], zs.at[3], zr.at[3], section(-3))

    def begin(i):
        @pl.loop(1, NB)
        def _(k):
            phase1(i, k).start()

        own1(i).start()

    def middle(i):
        own1(i).wait()

        @pl.loop(1, NB)
        def _(k):
            phase1(i, k).wait_recv()

        @pl.loop(0, NB)
        def _(t):
            for r in range(HALF):
                up = 2 * r + par
                own = off_ref[0, up] + t + NB
                above = (own - off_ref[0, jnp.minimum(up + 1, NU - 1)]) & (NB - 1)
                below = (own - off_ref[0, jnp.maximum(up - 1, 0)]) & (NB - 1)
                send_of[i][t, 0, r] = recv_of[i][above, r]
                send_of[i][t, 1, r] = recv_of[i][below, r]

        @pl.loop(1, NB)
        def _(k):
            phase2(i, k).start()

        own2(i).start()

    def end(i):
        own2(i).wait()

        @pl.loop(1, NB)
        def _(k):
            phase2(i, k).wait_recv()

    begin(0)

    @pl.when(odd)
    def _():
        direct(NC - FAR).start()
        hop(0).start()

    @pl.when(jnp.logical_not(odd))
    def _():
        direct(NC).start()

    for j in range(2):
        side(0, j).start()

    @pl.loop(1, NB)
    def _(k):
        tiny(0, k).start()

    ranks_all[me] = ranks[...]
    middle(0)

    def own_v(t):
        return xs[t // 2, t % 2]

    def source(i, c, t):
        if c == 1:
            at = jnp.maximum(t, 1)
            return wide_of[i][0, at // 2, at % 2]
        if c == 2:
            at = jnp.minimum(t + 2, NU)
            return wide_of[i][1, at // 2, at % 2]
        return side_of[i][c - 3][t // 2, t % 2]

    def first_source(c, t):
        return jnp.where(exists(off_ref, t, c), source(0, c, t), jnp.zeros((SB, SB), BF16))

    loaded(0)

    @pl.loop(0, NU, step=2)
    def _(t0):
        ts_ = [t0, t0 + 1]
        products(lv, rv, h0, [(0, t, own_v(t)) for t in ts_], True)

    for j in range(2):
        side(0, j).wait_recv()
    loaded(3)
    loaded(4)

    @pl.loop(0, NU)
    def _(t):
        products(lv, rv, h0, [(c, t, first_source(c, t)) for c in (3, 4)], False)

    end(0)
    loaded(1)
    loaded(2)

    @pl.loop(0, NU)
    def _(t):
        products(lv, rv, h0, [(c, t, first_source(c, t)) for c in (1, 2)], False)
        h = jnp.where(slot_mask(dims_ref[0, 0, t], dims_ref[0, 1, t]), h0[t], 0.0)
        v = own_v(t).astype(F32)
        n = total(v * v)
        p = total(v * h)
        alpha = jnp.where(n > 0.0, p / jnp.where(n > 0.0, n, 1.0), 0.0)
        g = h - alpha * v
        h0[t] = h
        gs[t // 2, t % 2] = g.astype(BF16)
        rest = total(g * g)
        rows = lax.broadcasted_iota(jnp.int32, (8, SB), 0)
        lanes = lax.broadcasted_iota(jnp.int32, (8, SB), 1)
        entry = jnp.where(rows == 0, n, jnp.where(rows == 1, p, jnp.where(rows == 2, rest, alpha)))
        sums[...] = jnp.where((lanes == t) & (rows < 4), entry, sums[...])

    @pl.loop(1, NB)
    def _(k):
        tiny(1, k).start()

    begin(1)
    for j in range(2):
        side(1, j).start()
    sums_all[me] = sums[...]

    @pl.when(odd)
    def _():
        hop(0).wait_recv()
        hop(1).start()

    @pl.loop(1, NB)
    def _(k):
        tiny(1, k).wait_recv()

    every = sums_all[...]
    nt, pt, rt, at = every[:, 0, :], every[:, 1, :], every[:, 2, :], every[:, 3, :]
    norm = total(nt)
    a0 = total(pt) / norm
    gap = at - a0
    beta = jnp.sqrt(total(rt + gap * gap * nt) / norm + 1e-6)
    scale = jnp.sqrt(CELLS / norm)
    kappa = scale / beta

    def second_source(c, t):
        alpha = far_entry(sums_all, source_device(off_ref, t, c), 3, source_slot(t, c))
        x = kappa * (source(1, c, t).astype(F32) + (alpha - a0) * source(0, c, t).astype(F32))
        x = jnp.where(exists(off_ref, t, c), x, 0.0).astype(BF16)
        vs[c - 1, t] = x
        return x

    middle(1)

    @pl.loop(0, NU, step=2)
    def _(t0):
        work = []
        for t in (t0, t0 + 1):
            x = (kappa * (h0[t] - a0 * own_v(t).astype(F32))).astype(BF16)
            v1[t] = x
            work.append((0, t, x))
        products(lv, rv, h1, work, True)

    for j in range(2):
        side(1, j).wait_recv()

    @pl.loop(0, NU)
    def _(t):
        products(lv, rv, h1, [(c, t, second_source(c, t)) for c in (3, 4)], False)

    end(1)
    qt[...] = jnp.zeros((8, SB), F32)

    @pl.loop(0, NU)
    def _(t):
        products(lv, rv, h1, [(c, t, second_source(c, t)) for c in (1, 2)], False)
        h = jnp.where(slot_mask(dims_ref[0, 0, t], dims_ref[0, 1, t]), h1[t], 0.0)
        h1[t] = h
        qt[0:1, :] += jnp.sum(v1[t].astype(F32) * h, axis=0, keepdims=True)

    @pl.loop(1, NB)
    def _(k):
        tiny(2, k).start()

    qt_all[me] = qt[...]

    @pl.when(odd)
    def _():
        hop(1).wait_recv()
        hop(2).start()

    @pl.loop(1, NB)
    def _(k):
        tiny(0, k).wait_recv()
        tiny(2, k).wait_recv()

    a1 = total(jnp.sum(qt_all[...], axis=0)) / CELLS
    half = (a0 - a1) / 2.0
    ritz = (a0 + a1) / 2.0 - jnp.sqrt(half * half + beta * beta)
    slip = ritz - a0
    length = jnp.sqrt(beta * beta + slip * slip)
    xcoef, ycoef = beta / length, slip / length
    coef_ref[...] = jnp.broadcast_to(ritz, (8, SB))
    lane = lax.broadcasted_iota(jnp.int32, (SB, SB), 1).astype(F32)

    def onward(c):
        return remote(kept.at[c], kept_ref.at[c], ks.at[c], kr.at[c], section(1))

    for c in range(5):

        @pl.loop(0, NU)
        def _(t):
            if c == 0:
                x = (xcoef * (own_v(t).astype(F32) * scale) + ycoef * v1[t].astype(F32)).astype(BF16)
                st[t] = x
                on = lane < far_entry(ranks_all, me, 0, t)
            else:
                x = xcoef * (source(0, c, t).astype(F32) * scale) + ycoef * vs[c - 1, t].astype(F32)
                rank = far_entry(ranks_all, source_device(off_ref, t, c), 0, source_slot(t, c))
                on = (lane < rank) & exists(off_ref, t, c)
            kept[c, t] = jnp.where(on, x.astype(F32), 0.0).astype(BF16)

        if c:
            onward(c - 1).start()

    @pl.loop(0, NU)
    def _(t):
        hst[t] = (xcoef * (h0[t] * scale) + ycoef * h1[t]).astype(BF16)

    onward(4).start()
    outs = [
        pltpu.make_async_copy(st, state_ref, fin.at[0]),
        pltpu.make_async_copy(hst, hstate_ref, fin.at[1]),
    ]
    for copy in outs:
        copy.start()

    for i in range(2):
        for j in range(2):
            side(i, j).wait_send()

    @pl.loop(1, NB)
    def _(k):
        for i in range(2):
            phase1(i, k).wait_send()
            phase2(i, k).wait_send()
        for i in range(3):
            tiny(i, k).wait_send()

    for copy in outs:
        copy.wait()

    @pl.when(odd)
    def _():
        direct(NC - FAR).wait_send()
        for i in range(3):
            hop(i).wait_send()
        direct(NC).wait_recv()

    @pl.when(jnp.logical_not(odd))
    def _():
        direct(NC).wait_send()
        direct(NC - FAR).wait_recv()
        hop(2).wait_recv()

    for c in range(5):
        onward(c).wait()


def main_call(nsec, offsets, dims, ranks, x, lenv, renv):
    pair = (HALF, 2, SB, SB)
    flat = (NU, SB, SB)
    tile, tiles = (8, SB), (NB, 8, SB)
    far = jax.ShapeDtypeStruct((FAR, NU, SB, SB), BF16)
    wide = pltpu.VMEM((2, HALF + 1, 2, SB, SB), BF16)
    bf = lambda *shape: pltpu.VMEM(shape, BF16)
    f32 = lambda *shape: pltpu.VMEM(shape, F32)
    dma = lambda *shape: pltpu.SemaphoreType.DMA(shape)
    return pl.pallas_call(
        functools.partial(main_kernel, nsec),
        out_shape=[
            jax.ShapeDtypeStruct((NC,) + flat, BF16),
            far,
            far,
            jax.ShapeDtypeStruct((5,) + flat, BF16),
            jax.ShapeDtypeStruct(flat, BF16),
            jax.ShapeDtypeStruct(flat, BF16),
            jax.ShapeDtypeStruct(tile, F32),
        ],
        in_specs=[SMEM_SPEC, SMEM_SPEC, SMEM_SPEC, VMEM_SPEC, ANY_SPEC, ANY_SPEC],
        out_specs=[ANY_SPEC] * 6 + [VMEM_SPEC],
        scratch_shapes=[
            bf(NC, *flat), bf(NC, *flat), bf(*pair), wide, bf(*pair), bf(*pair), bf(*pair), wide, bf(*pair), bf(*pair),
            bf(NB, HALF, ROWS, SB), bf(NB, HALF, ROWS, SB),
            bf(NB, 2, HALF, ROWS, SB), bf(NB, 2, HALF, ROWS, SB),
            f32(*flat), f32(*flat), bf(*flat), bf(4, *flat), bf(5, *flat), bf(*flat), bf(*flat),
            f32(*tile), f32(*tiles), f32(*tile), f32(*tiles), f32(*tile), f32(*tiles),
            dma(NC), dma(NC), dma(2, 2), dma(2, 2), dma(2, NB), dma(2, NB), dma(2, NB), dma(2, NB),
            dma(3, NB), dma(3, NB), dma(2, 2), dma(4), dma(4), dma(5), dma(5), dma(2),
        ],
        compiler_params=pltpu.CompilerParams(collective_id=0, has_side_effects=True),
        name="davidson",
    )(offsets, dims, ranks, x, lenv, renv)


def update_kernel(slots, head_ref, coef_ref, own_ref, l_ref, k_ref, si_ref, hi_ref, next_ref, s_ref, hs_ref, e_ref):
    first_section = head_ref[0] == 1
    s_ref[...] = si_ref[...]
    hs_ref[...] = hi_ref[...]
    e_ref[0] = coef_ref[0, 0]

    @pl.when(first_section)
    def _():
        next_ref[...] = own_ref[...]

    @pl.when(jnp.logical_not(first_section))
    def _():
        for i in range(slots):
            kept = k_ref[0, i]
            for c in range(5):
                stack = jnp.concatenate([l_ref[c + 5 * k, i] for k in range(PER)], axis=0)
                inner = jnp.dot(stack, k_ref[c, i], preferred_element_type=F32).astype(BF16)
                wide = jnp.concatenate([inner[k * SB : (k + 1) * SB] for k in range(PER)], axis=1)
                out = lax.dot_general(kept, wide, (((0,), (0,)), ((), ())), preferred_element_type=F32).astype(BF16)
                for k in range(PER):
                    next_ref[c + 5 * k, i] = out[:, k * SB : (k + 1) * SB]


SLOTS = 2


def update(head, coef, lenv, prev, kept, state, hstate):
    tile = pl.BlockSpec((8, SB), lambda t, *_: (0, 0))
    one = pl.BlockSpec((SLOTS, SB, SB), lambda t, *_: (t, 0, 0))
    env = (NC, SLOTS, SB, SB)
    own = pl.BlockSpec(env, lambda t, head: (0, t * head[0], 0, 0))
    far = pl.BlockSpec(env, lambda t, head: (0, t * (1 - head[0]), 0, 0))
    flat = jax.ShapeDtypeStruct((NU, SB, SB), BF16)
    return pl.pallas_call(
        functools.partial(update_kernel, SLOTS),
        grid_spec=pltpu.PrefetchScalarGridSpec(
            num_scalar_prefetch=1,
            grid=(NU // SLOTS,),
            in_specs=[tile, own, far, pl.BlockSpec((5, SLOTS, SB, SB), lambda t, *_: (0, t, 0, 0)), one, one],
            out_specs=[pl.BlockSpec(env, lambda t, *_: (0, t, 0, 0)), one, one, SMEM_SPEC],
        ),
        out_shape=[
            jax.ShapeDtypeStruct((NC, NU, SB, SB), BF16),
            flat,
            flat,
            jax.ShapeDtypeStruct((1,), F32),
        ],
        name="update",
    )(head, coef, lenv, prev, kept, state, hstate)


def shards(wavefunction, left_env, right_env, offsets, dims, ranks):
    nsec = lax.axis_size("sec")
    lenv, renv = left_env[0], right_env[0]
    prev, _, _, kept, state, hstate, coef = main_call(
        nsec, offsets, dims.transpose(0, 2, 1), ranks, wavefunction[0].reshape((HALF, 2, SB, SB)), lenv, renv
    )
    head = jnp.where(lax.axis_index("sec") == 0, 1, 0).astype(jnp.int32).reshape((1,))
    next_left, state, hstate, energy = update(head, coef, lenv, prev, kept, state, hstate)
    return state[None], hstate[None], energy, next_left[None]


def solution(mesh):
    placed = (
        P("sec", "blk", None, None),
        P("sec", None, "blk", None, None),
        P("sec", None, "blk", None, None),
        P("sec", None),
        P("sec", "blk", None),
        P("sec", "blk"),
    )
    return jax.shard_map(
        shards,
        mesh=mesh,
        in_specs=placed,
        out_specs=(
            P("sec", "blk", None, None),
            P("sec", "blk", None, None),
            P("sec"),
            P("sec", None, "blk", None, None),
        ),
        check_vma=False,
    )
```

time: 539 us -> 116 us (0.22)
  waiting for transfers between devices: 240 us -> 0 us
  blocking collectives: 114 us -> 0 us
  Pallas kernels: 0 us -> 113 us
  local copies, waits for them, and re-layouts: 85.8 us -> 0 us
  matrix products: 57 us -> 0 us
  other arithmetic: 18.8 us -> 0 us
  between operations: 18.8 us -> 0.65 us
    all_gather x3 -> x0, waiting for transfers between devices: 154 us -> none  [route_blocks(): whole = lax.all_gather(state, 'blk', axis=0, tiled=True)]
    psum x3 -> x0, blocking collectives: 114 us -> none  [the longest x1 39.3 us: shards(): a_one = lax.psum(jnp.sum(vone.astype(jnp.float32) * hone), 'blk') / cells]
    pallas_call x0 -> x2, Pallas kernels: none -> 113 us  [the longest x1 102 us: main_call(): pl.pallas_call(functools.partial(main_kernel, nsec), out_shape=[jax.Shape...]
    ppermute x1 -> x0, waiting for transfers between devices: 85.6 us -> none  [passed_along(): return lax.ppermute(value, axis, pairs)]
    dot_general x15 -> x0, matrix products: 57 us -> none  [the longest x10 37.5 us: apply_ham(): jnp.einsum('wtac,wtdc->tad', inner, renv[ctype::5], preferred_element_typ...]
    gather x12 -> x0, local copies, waits for them, and re-layouts: 40.9 us -> none  [route_blocks(): picked = [jnp.take(whole, entry, axis=0) for entry in indices]]
    squeeze x1 -> x0, local copies, waits for them, and re-layouts: 11.6 us -> none  [shards(): renv = right_env[0]]
    broadcast_in_dim x3 -> x0, other arithmetic: 11.4 us -> none  [the longest x1 9.42 us: shards(): next_left[None]]
  transfers between devices with their start and end apart: 4 -> 0, of which waited for: 4 -> 0; matrix products, arithmetic and copies ran while one was open for 5% -> 0% of each run, Pallas kernels for 0% -> 0%
where the time goes in v2:
time: 116 us; the launch traced here: 114 us
  Pallas kernels  113 us (97%)
    pallas_call x1, Pallas kernels, main_call(): pl.pallas_call(functools.partial(main_kernel, nsec), out_shape=[jax.Shape...  102 us
    pallas_call x1, Pallas kernels, update(): pl.pallas_call(functools.partial(update_kernel, SLOTS), grid_spec=pltpu.P...  11.2 us

profile of v2, /device:TPU:64, one launch (start us, length us, event | category | flops | bytes accessed | tf_op | source)
XLA Modules:
  0.0 113.9 jit_solution(1308255890911567004)
XLA Ops:
  0.6 102.1 %davidson.1 = (bf16[20,12,128,128]{3,2,1,0:T(8,128)(2,1)}, bf16[6,12,128,128]{3,2,1,0:T(8,128)(2,1)}, bf16[6,12,128,128]{3,2,1,0:T(8,128)(2,1)}, bf16[5,12,128,1...) custom-call(s32[1,12]{1,0:T(1,128)} %off_ref.1, ...), custom_call_target="tpu_custom_call" | custom-call | tf_op jit(solution)/shard_map/davidson/pallas_call | solution.py:465
  102.7 11.2 %update.1 = (bf16[20,12,128,128]{3,2,1,0:T(8,128)(2,1)}, bf16[12,128,128]{2,1,0:T(8,128)(2,1)}, bf16[12,128,128]{2,1,0:T(8,128)(2,1)}, f32[1]{0:T(128)}) custom-call(s32[1]{0:T(128)} %bitcast.head_ref, f32[8,128]{1,0:T(8,128)} %get-tuple-element.13.coef_ref, bf16[20,12,128,128]{3,2,1,0:T(8,128)(2,1)} %bitcast.9, ...), custom_call_target="tpu_custom_call" | custom-call | tf_op jit(solution)/shard_map/update/pallas_call | solution.py:525

commit v3 on v2

--- a/solution.py
+++ b/solution.py
@@ -21,17 +21,15 @@
 ROWS = 16
 NCH = SB // ROWS
 PER = NC // 5
-FAR = 6
+FAR = 5
 CELLS = float(NB * NU * SB * SB)
 
 
-def lane_tile(values):
-    row = lax.broadcasted_iota(jnp.int32, (8, SB), 0)
-    lane = lax.broadcasted_iota(jnp.int32, (8, SB), 1)
-    tile = jnp.zeros((8, SB), F32)
-    for i, entries in enumerate(values):
-        for u, entry in enumerate(entries):
-            tile = jnp.where((row == i) & (lane == u), entry, tile)
+def slot_tile(entries):
+    row = lax.broadcasted_iota(jnp.int32, (16, SB), 0)
+    tile = jnp.zeros((16, SB), F32)
+    for u, entry in enumerate(entries):
+        tile = jnp.where(row == u, entry, tile)
     return tile
 
 
@@ -69,12 +67,6 @@
 
 def total(x):
     return jnp.sum(jnp.sum(x, axis=0, keepdims=True), axis=1, keepdims=True)
-
-
-def far_entry(tiles_ref, device, row, slot):
-    lane = lax.broadcasted_iota(jnp.int32, (8, SB), 1)
-    rows = lax.broadcasted_iota(jnp.int32, (8, SB), 0)
-    return total(jnp.where((lane == slot) & (rows == row), tiles_ref[device], 0.0))
 
 
 def products(l_ref, r_ref, acc_ref, work, fresh):
@@ -99,7 +91,7 @@
     nsec, off_ref, dims_ref, rank_ref, x_ref, l_hbm, r_hbm,
     prev_ref, rel1, rel2, kept_ref, state_ref, hstate_ref, coef_ref,
     lv, rv, xs, va, v3, v4, gs, ga, g3, g4, recv_v, recv_g, send_v, send_g, h0, h1, v1, vs, kept, st, hst,
-    ranks, ranks_all, sums, sums_all, qt, qt_all,
+    ranks, ranks_all, sums, sums_all, qt, qt_all, part_n, part_p, part_r, alphas, alpha_all,
     l_sem, r_sem, side_s, side_r, p1s, p1r, p2s, p2r, ts, tr, loc, zs, zr, ks, kr, fin
 ):
     me = lax.axis_index("blk")
@@ -142,8 +134,9 @@
     for u in range(NU):
         on = slot_mask(dims_ref[0, 0, u], dims_ref[0, 1, u])
         xs[u // 2, u % 2] = jnp.where(on, x_ref[u // 2, u % 2], jnp.zeros((SB, SB), BF16))
-    ranks[...] = lane_tile([[rank_ref[0, u].astype(F32) for u in range(NU)]])
-    sums[...] = jnp.zeros((8, SB), F32)
+    ranks[...] = slot_tile([rank_ref[0, u].astype(F32) for u in range(NU)])
+    for ref in (part_n, part_p, part_r):
+        ref[...] = jnp.zeros((16, SB), F32)
     pl.semaphore_wait(barrier, NB + 5)
 
     state_of = (xs, gs)
@@ -269,8 +262,11 @@
 
     @pl.loop(0, NU, step=2)
     def _(t0):
-        ts_ = [t0, t0 + 1]
-        products(lv, rv, h0, [(0, t, own_v(t)) for t in ts_], True)
+        pair = [t0, t0 + 1]
+        products(lv, rv, h0, [(0, t, own_v(t)) for t in pair], True)
+        for t in pair:
+            v = own_v(t).astype(F32)
+            part_n[pl.ds(t, 1), :] = jnp.sum(v * v, axis=0, keepdims=True)
 
     for j in range(2):
         side(0, j).wait_recv()
@@ -285,28 +281,36 @@
     loaded(1)
     loaded(2)
 
-    @pl.loop(0, NU)
-    def _(t):
-        products(lv, rv, h0, [(c, t, first_source(c, t)) for c in (1, 2)], False)
-        h = jnp.where(slot_mask(dims_ref[0, 0, t], dims_ref[0, 1, t]), h0[t], 0.0)
-        v = own_v(t).astype(F32)
-        n = total(v * v)
-        p = total(v * h)
-        alpha = jnp.where(n > 0.0, p / jnp.where(n > 0.0, n, 1.0), 0.0)
-        g = h - alpha * v
-        h0[t] = h
-        gs[t // 2, t % 2] = g.astype(BF16)
-        rest = total(g * g)
-        rows = lax.broadcasted_iota(jnp.int32, (8, SB), 0)
-        lanes = lax.broadcasted_iota(jnp.int32, (8, SB), 1)
-        entry = jnp.where(rows == 0, n, jnp.where(rows == 1, p, jnp.where(rows == 2, rest, alpha)))
-        sums[...] = jnp.where((lanes == t) & (rows < 4), entry, sums[...])
+    @pl.loop(0, NU, step=2)
+    def _(t0):
+        pair = [t0, t0 + 1]
+        products(lv, rv, h0, [(c, t, first_source(c, t)) for t in pair for c in (1, 2)], False)
+        for t in pair:
+            h = jnp.where(slot_mask(dims_ref[0, 0, t], dims_ref[0, 1, t]), h0[t], 0.0)
+            h0[t] = h
+            part_p[pl.ds(t, 1), :] = jnp.sum(own_v(t).astype(F32) * h, axis=0, keepdims=True)
+
+    n_own = jnp.sum(part_n[...], axis=1, keepdims=True)
+    p_own = jnp.sum(part_p[...], axis=1, keepdims=True)
+    alpha_own = jnp.where(n_own > 0.0, p_own / jnp.where(n_own > 0.0, n_own, 1.0), 0.0)
+    alphas[...] = jnp.broadcast_to(alpha_own, (16, SB))
+
+    @pl.loop(0, NU, step=2)
+    def _(t0):
+        for t in (t0, t0 + 1):
+            g = h0[t] - alphas[pl.ds(t, 1), :] * own_v(t).astype(F32)
+            gs[t // 2, t % 2] = g.astype(BF16)
+            part_r[pl.ds(t, 1), :] = jnp.sum(g * g, axis=0, keepdims=True)
+
+    r_own = jnp.sum(part_r[...], axis=1, keepdims=True)
+    lanes = lax.broadcasted_iota(jnp.int32, (16, SB), 1)
+    sums[...] = jnp.where(lanes == 0, n_own, jnp.where(lanes == 1, p_own, jnp.where(lanes == 2, r_own, alpha_own)))
+    begin(1)
 
     @pl.loop(1, NB)
     def _(k):
         tiny(1, k).start()
 
-    begin(1)
     for j in range(2):
         side(1, j).start()
     sums_all[me] = sums[...]
@@ -321,16 +325,18 @@
         tiny(1, k).wait_recv()
 
     every = sums_all[...]
-    nt, pt, rt, at = every[:, 0, :], every[:, 1, :], every[:, 2, :], every[:, 3, :]
-    norm = total(nt)
-    a0 = total(pt) / norm
+    place = lax.broadcasted_iota(jnp.int32, (NB, 16, SB), 2)
+    nt, pt, rt, at = [jnp.sum(jnp.where(place == i, every, 0.0), axis=2, keepdims=True) for i in range(4)]
+    alpha_all[...] = jnp.broadcast_to(at, (NB, 16, SB))
+    norm = total(jnp.sum(nt, axis=0))
+    a0 = total(jnp.sum(pt, axis=0)) / norm
     gap = at - a0
-    beta = jnp.sqrt(total(rt + gap * gap * nt) / norm + 1e-6)
+    beta = jnp.sqrt(total(jnp.sum(rt + gap * gap * nt, axis=0)) / norm + 1e-6)
     scale = jnp.sqrt(CELLS / norm)
     kappa = scale / beta
 
     def second_source(c, t):
-        alpha = far_entry(sums_all, source_device(off_ref, t, c), 3, source_slot(t, c))
+        alpha = alpha_all[source_device(off_ref, t, c), pl.ds(source_slot(t, c), 1), :]
         x = kappa * (source(1, c, t).astype(F32) + (alpha - a0) * source(0, c, t).astype(F32))
         x = jnp.where(exists(off_ref, t, c), x, 0.0).astype(BF16)
         vs[c - 1, t] = x
@@ -357,12 +363,14 @@
     end(1)
     qt[...] = jnp.zeros((8, SB), F32)
 
-    @pl.loop(0, NU)
-    def _(t):
-        products(lv, rv, h1, [(c, t, second_source(c, t)) for c in (1, 2)], False)
-        h = jnp.where(slot_mask(dims_ref[0, 0, t], dims_ref[0, 1, t]), h1[t], 0.0)
-        h1[t] = h
-        qt[0:1, :] += jnp.sum(v1[t].astype(F32) * h, axis=0, keepdims=True)
+    @pl.loop(0, NU, step=2)
+    def _(t0):
+        pair = [t0, t0 + 1]
+        products(lv, rv, h1, [(c, t, second_source(c, t)) for t in pair for c in (1, 2)], False)
+        for t in pair:
+            h = jnp.where(slot_mask(dims_ref[0, 0, t], dims_ref[0, 1, t]), h1[t], 0.0)
+            h1[t] = h
+            qt[0:1, :] += jnp.sum(v1[t].astype(F32) * h, axis=0, keepdims=True)
 
     @pl.loop(1, NB)
     def _(k):
@@ -387,33 +395,36 @@
     length = jnp.sqrt(beta * beta + slip * slip)
     xcoef, ycoef = beta / length, slip / length
     coef_ref[...] = jnp.broadcast_to(ritz, (8, SB))
-    lane = lax.broadcasted_iota(jnp.int32, (SB, SB), 1).astype(F32)
+    lane = lax.broadcasted_iota(jnp.int32, (1, SB), 1).astype(F32)
+    v_coef = xcoef * scale
 
     def onward(c):
         return remote(kept.at[c], kept_ref.at[c], ks.at[c], kr.at[c], section(1))
 
     for c in range(5):
 
-        @pl.loop(0, NU)
-        def _(t):
-            if c == 0:
-                x = (xcoef * (own_v(t).astype(F32) * scale) + ycoef * v1[t].astype(F32)).astype(BF16)
-                st[t] = x
-                on = lane < far_entry(ranks_all, me, 0, t)
-            else:
-                x = xcoef * (source(0, c, t).astype(F32) * scale) + ycoef * vs[c - 1, t].astype(F32)
-                rank = far_entry(ranks_all, source_device(off_ref, t, c), 0, source_slot(t, c))
-                on = (lane < rank) & exists(off_ref, t, c)
-            kept[c, t] = jnp.where(on, x.astype(F32), 0.0).astype(BF16)
+        @pl.loop(0, NU, step=2)
+        def _(t0):
+            for t in (t0, t0 + 1):
+                if c == 0:
+                    x = (v_coef * own_v(t).astype(F32) + ycoef * v1[t].astype(F32)).astype(BF16)
+                    st[t] = x
+                    on = lane < ranks[pl.ds(t, 1), :]
+                else:
+                    x = v_coef * source(0, c, t).astype(F32) + ycoef * vs[c - 1, t].astype(F32)
+                    rank = ranks_all[source_device(off_ref, t, c), pl.ds(source_slot(t, c), 1), :]
+                    on = (lane < rank) & exists(off_ref, t, c)
+                kept[c, t] = jnp.where(on, x.astype(F32), 0.0).astype(BF16)
 
         if c:
             onward(c - 1).start()
 
+    onward(4).start()
+
     @pl.loop(0, NU)
     def _(t):
-        hst[t] = (xcoef * (h0[t] * scale) + ycoef * h1[t]).astype(BF16)
-
-    onward(4).start()
+        hst[t] = (v_coef * h0[t] + ycoef * h1[t]).astype(BF16)
+
     outs = [
         pltpu.make_async_copy(st, state_ref, fin.at[0]),
         pltpu.make_async_copy(hst, hstate_ref, fin.at[1]),
@@ -456,7 +467,7 @@
 def main_call(nsec, offsets, dims, ranks, x, lenv, renv):
     pair = (HALF, 2, SB, SB)
     flat = (NU, SB, SB)
-    tile, tiles = (8, SB), (NB, 8, SB)
+    tile, slots = (8, SB), (16, SB)
     far = jax.ShapeDtypeStruct((FAR, NU, SB, SB), BF16)
     wide = pltpu.VMEM((2, HALF + 1, 2, SB, SB), BF16)
     bf = lambda *shape: pltpu.VMEM(shape, BF16)
@@ -480,7 +491,8 @@
             bf(NB, HALF, ROWS, SB), bf(NB, HALF, ROWS, SB),
             bf(NB, 2, HALF, ROWS, SB), bf(NB, 2, HALF, ROWS, SB),
             f32(*flat), f32(*flat), bf(*flat), bf(4, *flat), bf(5, *flat), bf(*flat), bf(*flat),
-            f32(*tile), f32(*tiles), f32(*tile), f32(*tiles), f32(*tile), f32(*tiles),
+            f32(*slots), f32(NB, *slots), f32(*slots), f32(NB, *slots), f32(*tile), f32(NB, *tile),
+            f32(*slots), f32(*slots), f32(*slots), f32(*slots), f32(NB, *slots),
             dma(NC), dma(NC), dma(2, 2), dma(2, 2), dma(2, NB), dma(2, NB), dma(2, NB), dma(2, NB),
             dma(3, NB), dma(3, NB), dma(2, 2), dma(4), dma(4), dma(5), dma(5), dma(2),
         ],

time: 116 us -> 109 us (0.940)
  Pallas kernels: 113 us -> 106 us
    pallas_call x1, Pallas kernels: 102 us -> 95.2 us  [main_call(): pl.pallas_call(functools.partial(main_kernel, nsec), out_shape=[jax.Shape...]
where the time goes in v3:
time: 109 us; the launch traced here: 107 us
  Pallas kernels  106 us (97%)
    pallas_call x1, Pallas kernels, main_call(): pl.pallas_call(functools.partial(main_kernel, nsec), out_shape=[jax.Shape...  95.2 us
    pallas_call x1, Pallas kernels, update(): pl.pallas_call(functools.partial(update_kernel, SLOTS), grid_spec=pltpu.P...  11.1 us

profile of v3, /device:TPU:64, one launch (start us, length us, event | category | flops | bytes accessed | tf_op | source)
XLA Modules:
  0.0 106.9 jit_solution(591419642104060116)
XLA Ops:
  0.6 95.2 %davidson.1 = (bf16[20,12,128,128]{3,2,1,0:T(8,128)(2,1)}, bf16[5,12,128,128]{3,2,1,0:T(8,128)(2,1)}, bf16[5,12,128,128]{3,2,1,0:T(8,128)(2,1)}, bf16[5,12,128,1...) custom-call(s32[1,12]{1,0:T(1,128)} %off_ref.1, ...), custom_call_target="tpu_custom_call" | custom-call | tf_op jit(solution)/shard_map/davidson/pallas_call | solution.py:476
  95.8 11.1 %update.1 = (bf16[20,12,128,128]{3,2,1,0:T(8,128)(2,1)}, bf16[12,128,128]{2,1,0:T(8,128)(2,1)}, bf16[12,128,128]{2,1,0:T(8,128)(2,1)}, f32[1]{0:T(128)}) custom-call(s32[1]{0:T(128)} %bitcast.head_ref, f32[8,128]{1,0:T(8,128)} %get-tuple-element.13.coef_ref, bf16[20,12,128,128]{3,2,1,0:T(8,128)(2,1)} %bitcast.9, ...), custom_call_target="tpu_custom_call" | custom-call | tf_op jit(solution)/shard_map/update/pallas_call | solution.py:537

commit v4 on v3

--- a/solution.py
+++ b/solution.py
@@ -89,10 +89,10 @@
 
 def main_kernel(
     nsec, off_ref, dims_ref, rank_ref, x_ref, l_hbm, r_hbm,
-    prev_ref, rel1, rel2, kept_ref, state_ref, hstate_ref, coef_ref,
+    prev_ref, rel1, rel2, kept_ref, flag_ref, state_ref, hstate_ref, coef_ref,
     lv, rv, xs, va, v3, v4, gs, ga, g3, g4, recv_v, recv_g, send_v, send_g, h0, h1, v1, vs, kept, st, hst,
-    ranks, ranks_all, sums, sums_all, qt, qt_all, part_n, part_p, part_r, alphas, alpha_all,
-    l_sem, r_sem, side_s, side_r, p1s, p1r, p2s, p2r, ts, tr, loc, zs, zr, ks, kr, fin
+    ranks, ranks_all, sums, sums_all, qt, qt_all, part_n, part_p, part_r, alphas, alpha_all, flags,
+    l_sem, r_sem, side_s, side_r, p1s, p1r, p2s, p2r, ts, tr, loc, zs, zr, ks, kr, fs, fr, fin
 ):
     me = lax.axis_index("blk")
     sec = lax.axis_index("sec")
@@ -135,6 +135,10 @@
         on = slot_mask(dims_ref[0, 0, u], dims_ref[0, 1, u])
         xs[u // 2, u % 2] = jnp.where(on, x_ref[u // 2, u % 2], jnp.zeros((SB, SB), BF16))
     ranks[...] = slot_tile([rank_ref[0, u].astype(F32) for u in range(NU)])
+    down = [jnp.where(exists(off_ref, u, 3), 1.0, 0.0) for u in range(NU)]
+    above_it = [jnp.where(exists(off_ref, u, 4), 1.0, 0.0) for u in range(NU)]
+    line = lax.broadcasted_iota(jnp.int32, (16, SB), 1)
+    flags[...] = jnp.where(line == 0, slot_tile(down), slot_tile(above_it))
     for ref in (part_n, part_p, part_r):
         ref[...] = jnp.zeros((16, SB), F32)
     pl.semaphore_wait(barrier, NB + 5)
@@ -177,6 +181,7 @@
         return remote(l_hbm.at[part], prev_ref.at[part], zs.at[0], zr.at[0], section(1))
 
     far = pl.ds(NC - FAR, FAR)
+    flag_copy = remote(flags, flag_ref, ks.at[3], kr.at[3], section(1))
 
     def hop(i):
         if i == 0:
@@ -240,6 +245,7 @@
     def _(k):
         tiny(0, k).start()
 
+    flag_copy.start()
     ranks_all[me] = ranks[...]
     middle(0)
 
@@ -290,6 +296,11 @@
             h0[t] = h
             part_p[pl.ds(t, 1), :] = jnp.sum(own_v(t).astype(F32) * h, axis=0, keepdims=True)
 
+    @pl.when(odd)
+    def _():
+        hop(0).wait_recv()
+        hop(1).start()
+
     n_own = jnp.sum(part_n[...], axis=1, keepdims=True)
     p_own = jnp.sum(part_p[...], axis=1, keepdims=True)
     alpha_own = jnp.where(n_own > 0.0, p_own / jnp.where(n_own > 0.0, n_own, 1.0), 0.0)
@@ -314,11 +325,6 @@
     for j in range(2):
         side(1, j).start()
     sums_all[me] = sums[...]
-
-    @pl.when(odd)
-    def _():
-        hop(0).wait_recv()
-        hop(1).start()
 
     @pl.loop(1, NB)
     def _(k):
@@ -339,7 +345,8 @@
         alpha = alpha_all[source_device(off_ref, t, c), pl.ds(source_slot(t, c), 1), :]
         x = kappa * (source(1, c, t).astype(F32) + (alpha - a0) * source(0, c, t).astype(F32))
         x = jnp.where(exists(off_ref, t, c), x, 0.0).astype(BF16)
-        vs[c - 1, t] = x
+        if c < 3:
+            vs[c - 1, t] = x
         return x
 
     middle(1)
@@ -361,6 +368,12 @@
         products(lv, rv, h1, [(c, t, second_source(c, t)) for c in (3, 4)], False)
 
     end(1)
+
+    @pl.when(odd)
+    def _():
+        hop(1).wait_recv()
+        hop(2).start()
+
     qt[...] = jnp.zeros((8, SB), F32)
 
     @pl.loop(0, NU, step=2)
@@ -377,11 +390,6 @@
         tiny(2, k).start()
 
     qt_all[me] = qt[...]
-
-    @pl.when(odd)
-    def _():
-        hop(1).wait_recv()
-        hop(2).start()
 
     @pl.loop(1, NB)
     def _(k):
@@ -401,7 +409,10 @@
     def onward(c):
         return remote(kept.at[c], kept_ref.at[c], ks.at[c], kr.at[c], section(1))
 
-    for c in range(5):
+    def forward(j):
+        return remote(kept_ref.at[0], kept_ref.at[3 + j], fs.at[j], fr.at[j], peer((1, NB - 1)[j]))
+
+    for c in range(3):
 
         @pl.loop(0, NU, step=2)
         def _(t0):
@@ -419,7 +430,7 @@
         if c:
             onward(c - 1).start()
 
-    onward(4).start()
+    onward(2).start()
 
     @pl.loop(0, NU)
     def _(t):
@@ -431,6 +442,9 @@
     ]
     for copy in outs:
         copy.start()
+    onward(0).wait_recv()
+    for j in range(2):
+        forward(j).start()
 
     for i in range(2):
         for j in range(2):
@@ -460,8 +474,12 @@
         direct(NC - FAR).wait_recv()
         hop(2).wait_recv()
 
-    for c in range(5):
+    onward(0).wait_send()
+    for c in (1, 2):
         onward(c).wait()
+    flag_copy.wait()
+    for j in range(2):
+        forward(j).wait()
 
 
 def main_call(nsec, offsets, dims, ranks, x, lenv, renv):
@@ -480,28 +498,29 @@
             far,
             far,
             jax.ShapeDtypeStruct((5,) + flat, BF16),
+            jax.ShapeDtypeStruct(slots, F32),
             jax.ShapeDtypeStruct(flat, BF16),
             jax.ShapeDtypeStruct(flat, BF16),
             jax.ShapeDtypeStruct(tile, F32),
         ],
         in_specs=[SMEM_SPEC, SMEM_SPEC, SMEM_SPEC, VMEM_SPEC, ANY_SPEC, ANY_SPEC],
-        out_specs=[ANY_SPEC] * 6 + [VMEM_SPEC],
+        out_specs=[ANY_SPEC] * 7 + [VMEM_SPEC],
         scratch_shapes=[
             bf(NC, *flat), bf(NC, *flat), bf(*pair), wide, bf(*pair), bf(*pair), bf(*pair), wide, bf(*pair), bf(*pair),
             bf(NB, HALF, ROWS, SB), bf(NB, HALF, ROWS, SB),
             bf(NB, 2, HALF, ROWS, SB), bf(NB, 2, HALF, ROWS, SB),
-            f32(*flat), f32(*flat), bf(*flat), bf(4, *flat), bf(5, *flat), bf(*flat), bf(*flat),
+            f32(*flat), f32(*flat), bf(*flat), bf(2, *flat), bf(3, *flat), bf(*flat), bf(*flat),
             f32(*slots), f32(NB, *slots), f32(*slots), f32(NB, *slots), f32(*tile), f32(NB, *tile),
-            f32(*slots), f32(*slots), f32(*slots), f32(*slots), f32(NB, *slots),
+            f32(*slots), f32(*slots), f32(*slots), f32(*slots), f32(NB, *slots), f32(*slots),
             dma(NC), dma(NC), dma(2, 2), dma(2, 2), dma(2, NB), dma(2, NB), dma(2, NB), dma(2, NB),
-            dma(3, NB), dma(3, NB), dma(2, 2), dma(4), dma(4), dma(5), dma(5), dma(2),
+            dma(3, NB), dma(3, NB), dma(2, 2), dma(4), dma(4), dma(4), dma(4), dma(2), dma(2), dma(2),
         ],
         compiler_params=pltpu.CompilerParams(collective_id=0, has_side_effects=True),
         name="davidson",
     )(offsets, dims, ranks, x, lenv, renv)
 
 
-def update_kernel(slots, head_ref, coef_ref, own_ref, l_ref, k_ref, si_ref, hi_ref, next_ref, s_ref, hs_ref, e_ref):
+def update_kernel(slots, head_ref, flag_ref, coef_ref, own_ref, l_ref, k_ref, si_ref, hi_ref, next_ref, s_ref, hs_ref, e_ref):
     first_section = head_ref[0] == 1
     s_ref[...] = si_ref[...]
     hs_ref[...] = hi_ref[...]
@@ -517,7 +536,10 @@
             kept = k_ref[0, i]
             for c in range(5):
                 stack = jnp.concatenate([l_ref[c + 5 * k, i] for k in range(PER)], axis=0)
-                inner = jnp.dot(stack, k_ref[c, i], preferred_element_type=F32).astype(BF16)
+                x = k_ref[c, i]
+                if c > 2:
+                    x = jnp.where(flag_ref[pl.program_id(0) * slots + i, c - 3] > 0.5, x, jnp.zeros_like(x))
+                inner = jnp.dot(stack, x, preferred_element_type=F32).astype(BF16)
                 wide = jnp.concatenate([inner[k * SB : (k + 1) * SB] for k in range(PER)], axis=1)
                 out = lax.dot_general(kept, wide, (((0,), (0,)), ((), ())), preferred_element_type=F32).astype(BF16)
                 for k in range(PER):
@@ -527,7 +549,7 @@
 SLOTS = 2
 
 
-def update(head, coef, lenv, prev, kept, state, hstate):
+def update(head, flags, coef, lenv, prev, kept, state, hstate):
     tile = pl.BlockSpec((8, SB), lambda t, *_: (0, 0))
     one = pl.BlockSpec((SLOTS, SB, SB), lambda t, *_: (t, 0, 0))
     env = (NC, SLOTS, SB, SB)
@@ -539,7 +561,7 @@
         grid_spec=pltpu.PrefetchScalarGridSpec(
             num_scalar_prefetch=1,
             grid=(NU // SLOTS,),
-            in_specs=[tile, own, far, pl.BlockSpec((5, SLOTS, SB, SB), lambda t, *_: (0, t, 0, 0)), one, one],
+            in_specs=[SMEM_SPEC, tile, own, far, pl.BlockSpec((5, SLOTS, SB, SB), lambda t, *_: (0, t, 0, 0)), one, one],
             out_specs=[pl.BlockSpec(env, lambda t, *_: (0, t, 0, 0)), one, one, SMEM_SPEC],
         ),
         out_shape=[
@@ -549,17 +571,17 @@
             jax.ShapeDtypeStruct((1,), F32),
         ],
         name="update",
-    )(head, coef, lenv, prev, kept, state, hstate)
+    )(head, flags, coef, lenv, prev, kept, state, hstate)
 
 
 def shards(wavefunction, left_env, right_env, offsets, dims, ranks):
     nsec = lax.axis_size("sec")
     lenv, renv = left_env[0], right_env[0]
-    prev, _, _, kept, state, hstate, coef = main_call(
+    prev, _, _, kept, flags, state, hstate, coef = main_call(
         nsec, offsets, dims.transpose(0, 2, 1), ranks, wavefunction[0].reshape((HALF, 2, SB, SB)), lenv, renv
     )
     head = jnp.where(lax.axis_index("sec") == 0, 1, 0).astype(jnp.int32).reshape((1,))
-    next_left, state, hstate, energy = update(head, coef, lenv, prev, kept, state, hstate)
+    next_left, state, hstate, energy = update(head, flags, coef, lenv, prev, kept, state, hstate)
     return state[None], hstate[None], energy, next_left[None]
 
 

time: 109 us -> 102 us (0.936)
  Pallas kernels: 106 us -> 99.3 us
    pallas_call x1, Pallas kernels: 95.2 us -> 88.1 us  [main_call(): pl.pallas_call(functools.partial(main_kernel, nsec), out_shape=[jax.Shape...]
where the time goes in v4:
time: 102 us; the launch traced here: 99.9 us
  Pallas kernels  99.3 us (97%)
    pallas_call x1, Pallas kernels, main_call(): pl.pallas_call(functools.partial(main_kernel, nsec), out_shape=[jax.Shape...  88.1 us
    pallas_call x1, Pallas kernels, update(): pl.pallas_call(functools.partial(update_kernel, SLOTS), grid_spec=pltpu.P...  11.2 us

profile of v4, /device:TPU:64, one launch (start us, length us, event | category | flops | bytes accessed | tf_op | source)
XLA Modules:
  0.0 99.9 jit_solution(15639735877823105368)
XLA Ops:
  0.6 88.1 %davidson.1 = (bf16[20,12,128,128]{3,2,1,0:T(8,128)(2,1)}, bf16[5,12,128,128]{3,2,1,0:T(8,128)(2,1)}, bf16[5,12,128,128]{3,2,1,0:T(8,128)(2,1)}, bf16[5,12,128,1...) custom-call(s32[1,12]{1,0:T(1,128)} %off_ref.1, ...), custom_call_target="tpu_custom_call" | custom-call | tf_op jit(solution)/shard_map/davidson/pallas_call | solution.py:494
  88.8 11.2 %update.1 = (bf16[20,12,128,128]{3,2,1,0:T(8,128)(2,1)}, bf16[12,128,128]{2,1,0:T(8,128)(2,1)}, bf16[12,128,128]{2,1,0:T(8,128)(2,1)}, f32[1]{0:T(128)}) custom-call(s32[1]{0:T(128)} %bitcast.head_ref, f32[16,128]{1,0:T(8,128)} %get-tuple-element.14.flag_ref, f32[8,128]{1,0:T(8,128)} %get-tuple-element.15.coef_ref, bf16[20,12,128,128]{3,2,1,0:T(8,128)(2,1)} %bitcast.9, ...), custom_call_target="tpu_custom_call" | custom-call | tf_op jit(solution)/shard_map/update/pallas_call | solution.py:559

commit v5 on v4

--- a/solution.py
+++ b/solution.py
@@ -21,7 +21,7 @@
 ROWS = 16
 NCH = SB // ROWS
 PER = NC // 5
-FAR = 5
+FAR = 6
 CELLS = float(NB * NU * SB * SB)
 
 
@@ -520,58 +520,120 @@
     )(offsets, dims, ranks, x, lenv, renv)
 
 
-def update_kernel(slots, head_ref, flag_ref, coef_ref, own_ref, l_ref, k_ref, si_ref, hi_ref, next_ref, s_ref, hs_ref, e_ref):
-    first_section = head_ref[0] == 1
-    s_ref[...] = si_ref[...]
-    hs_ref[...] = hi_ref[...]
+def update_kernel(
+    flag_ref, coef_ref, l_hbm, prev_hbm, kept_hbm, state_hbm, hstate_hbm, next_hbm, s_hbm, hs_hbm, e_ref,
+    lp, kp, out, st, hst, l_sem, k_sem, o_sem, s_sem
+):
+    first_section = lax.axis_index("sec") == 0
+
+    def fetch(src, t):
+        return pltpu.make_async_copy(src.at[:, t], lp.at[:, t], l_sem.at[t])
+
+    def fetch_kept(t):
+        return pltpu.make_async_copy(kept_hbm.at[:, t], kp.at[:, t], k_sem.at[t])
+
+    def write(src, t):
+        return pltpu.make_async_copy(src.at[:, t], next_hbm.at[:, t], o_sem.at[t])
+
+    states = [(state_hbm, st, s_hbm), (hstate_hbm, hst, hs_hbm)]
+    takes = [pltpu.make_async_copy(src, at, s_sem.at[i]) for i, (src, at, _) in enumerate(states)]
+    gives = [pltpu.make_async_copy(at, dst, s_sem.at[2 + i]) for i, (_, at, dst) in enumerate(states)]
+
+    @pl.when(first_section)
+    def _():
+        @pl.loop(0, NU)
+        def _(t):
+            fetch(l_hbm, t).start()
+
+    @pl.when(jnp.logical_not(first_section))
+    def _():
+        @pl.loop(0, NU)
+        def _(t):
+            fetch_kept(t).start()
+            fetch(prev_hbm, t).start()
+
+    for copy in takes:
+        copy.start()
     e_ref[0] = coef_ref[0, 0]
 
     @pl.when(first_section)
     def _():
-        next_ref[...] = own_ref[...]
+        @pl.loop(0, NU)
+        def _(t):
+            fetch(l_hbm, t).wait()
+            write(lp, t).start()
+
+        for take, give in zip(takes, gives):
+            take.wait()
+            give.start()
+
+        @pl.loop(0, NU)
+        def _(t):
+            write(lp, t).wait()
 
     @pl.when(jnp.logical_not(first_section))
     def _():
-        for i in range(slots):
-            kept = k_ref[0, i]
+        def one(t):
+            kept = kp[0, t]
             for c in range(5):
-                stack = jnp.concatenate([l_ref[c + 5 * k, i] for k in range(PER)], axis=0)
-                x = k_ref[c, i]
+                stack = jnp.concatenate([lp[c + 5 * k, t] for k in range(PER)], axis=0)
+                x = kp[c, t]
                 if c > 2:
-                    x = jnp.where(flag_ref[pl.program_id(0) * slots + i, c - 3] > 0.5, x, jnp.zeros_like(x))
+                    x = jnp.where(flag_ref[t, c - 3] > 0.5, x, jnp.zeros_like(x))
                 inner = jnp.dot(stack, x, preferred_element_type=F32).astype(BF16)
                 wide = jnp.concatenate([inner[k * SB : (k + 1) * SB] for k in range(PER)], axis=1)
-                out = lax.dot_general(kept, wide, (((0,), (0,)), ((), ())), preferred_element_type=F32).astype(BF16)
+                new = lax.dot_general(kept, wide, (((0,), (0,)), ((), ())), preferred_element_type=F32).astype(BF16)
                 for k in range(PER):
-                    next_ref[c + 5 * k, i] = out[:, k * SB : (k + 1) * SB]
-
-
-SLOTS = 2
-
-
-def update(head, flags, coef, lenv, prev, kept, state, hstate):
-    tile = pl.BlockSpec((8, SB), lambda t, *_: (0, 0))
-    one = pl.BlockSpec((SLOTS, SB, SB), lambda t, *_: (t, 0, 0))
-    env = (NC, SLOTS, SB, SB)
-    own = pl.BlockSpec(env, lambda t, head: (0, t * head[0], 0, 0))
-    far = pl.BlockSpec(env, lambda t, head: (0, t * (1 - head[0]), 0, 0))
-    flat = jax.ShapeDtypeStruct((NU, SB, SB), BF16)
+                    out[c + 5 * k, t] = new[:, k * SB : (k + 1) * SB]
+
+        @pl.loop(0, NU)
+        def _(t):
+            fetch_kept(t).wait()
+            fetch(prev_hbm, t).wait()
+            one(t)
+
+            @pl.when(t > 0)
+            def _():
+                write(out, t - 1).start()
+
+        for take, give in zip(takes, gives):
+            take.wait()
+            give.start()
+        write(out, NU - 1).start()
+
+        @pl.loop(0, NU)
+        def _(t):
+            write(out, t).wait()
+
+    for give in gives:
+        give.wait()
+
+
+def update(flags, coef, lenv, prev, kept, state, hstate):
+    flat = (NU, SB, SB)
     return pl.pallas_call(
-        functools.partial(update_kernel, SLOTS),
-        grid_spec=pltpu.PrefetchScalarGridSpec(
-            num_scalar_prefetch=1,
-            grid=(NU // SLOTS,),
-            in_specs=[SMEM_SPEC, tile, own, far, pl.BlockSpec((5, SLOTS, SB, SB), lambda t, *_: (0, t, 0, 0)), one, one],
-            out_specs=[pl.BlockSpec(env, lambda t, *_: (0, t, 0, 0)), one, one, SMEM_SPEC],
-        ),
+        update_kernel,
+        in_specs=[SMEM_SPEC, SMEM_SPEC] + [ANY_SPEC] * 5,
+        out_specs=[ANY_SPEC] * 3 + [SMEM_SPEC],
         out_shape=[
-            jax.ShapeDtypeStruct((NC, NU, SB, SB), BF16),
-            flat,
-            flat,
+            jax.ShapeDtypeStruct((NC,) + flat, BF16),
+            jax.ShapeDtypeStruct(flat, BF16),
+            jax.ShapeDtypeStruct(flat, BF16),
             jax.ShapeDtypeStruct((1,), F32),
         ],
+        scratch_shapes=[
+            pltpu.VMEM((NC,) + flat, BF16),
+            pltpu.VMEM((5,) + flat, BF16),
+            pltpu.VMEM((NC,) + flat, BF16),
+            pltpu.VMEM(flat, BF16),
+            pltpu.VMEM(flat, BF16),
+            pltpu.SemaphoreType.DMA((NU,)),
+            pltpu.SemaphoreType.DMA((NU,)),
+            pltpu.SemaphoreType.DMA((NU,)),
+            pltpu.SemaphoreType.DMA((4,)),
+        ],
         name="update",
-    )(head, flags, coef, lenv, prev, kept, state, hstate)
+    )(flags, coef, lenv, prev, kept, state, hstate)
 
 
 def shards(wavefunction, left_env, right_env, offsets, dims, ranks):
@@ -580,8 +642,7 @@
     prev, _, _, kept, flags, state, hstate, coef = main_call(
         nsec, offsets, dims.transpose(0, 2, 1), ranks, wavefunction[0].reshape((HALF, 2, SB, SB)), lenv, renv
     )
-    head = jnp.where(lax.axis_index("sec") == 0, 1, 0).astype(jnp.int32).reshape((1,))
-    next_left, state, hstate, energy = update(head, flags, coef, lenv, prev, kept, state, hstate)
+    next_left, state, hstate, energy = update(flags, coef, lenv, prev, kept, state, hstate)
     return state[None], hstate[None], energy, next_left[None]
 
 

time: 102 us -> 107 us (1.049)
  Pallas kernels: 99.3 us -> 105 us
    pallas_call x1, Pallas kernels: 88.1 us -> 93.5 us  [main_call(): pl.pallas_call(functools.partial(main_kernel, nsec), out_shape=[jax.Shape...]
where the time goes in v5:
time: 107 us; the launch traced here: 106 us
  Pallas kernels  105 us (98%)
    pallas_call x1, Pallas kernels, main_call(): pl.pallas_call(functools.partial(main_kernel, nsec), out_shape=[jax.Shape...  93.5 us
    pallas_call x1, Pallas kernels, update(): pl.pallas_call(update_kernel, in_specs=[SMEM_SPEC, SMEM_SPEC] + [ANY_SPEC...  11.8 us

profile of v5, /device:TPU:64, one launch (start us, length us, event | category | flops | bytes accessed | tf_op | source)
XLA Modules:
  0.0 105.9 jit_solution(9798794147261508380)
XLA Ops:
  0.6 93.5 %davidson.1 = (bf16[20,12,128,128]{3,2,1,0:T(8,128)(2,1)}, bf16[6,12,128,128]{3,2,1,0:T(8,128)(2,1)}, bf16[6,12,128,128]{3,2,1,0:T(8,128)(2,1)}, bf16[5,12,128,1...) custom-call(s32[1,12]{1,0:T(1,128)} %off_ref.1, ...), custom_call_target="tpu_custom_call" | custom-call | tf_op jit(solution)/shard_map/davidson/pallas_call | solution.py:494
  94.2 11.8 %update.1 = (bf16[20,12,128,128]{3,2,1,0:T(8,128)(2,1)}, bf16[12,128,128]{2,1,0:T(8,128)(2,1)}, bf16[12,128,128]{2,1,0:T(8,128)(2,1)}, f32[1]{0:T(128)}) custom-call(f32[16,128]{1,0:T(8,128)} %get-tuple-element.14.flag_ref, f32[8,128]{1,0:T(8,128)} %get-tuple-element.15.coef_ref, bf16[20,12,128,128]{3,2,1,0:T(8,128)(2,1)} %bitcast.8, ...), custom_call_target="tpu_custom_call" | custom-call | tf_op jit(solution)/shard_map/update/pallas_call | solution.py:614

commit v6 on v5

--- a/solution.py
+++ b/solution.py
@@ -21,7 +21,9 @@
 ROWS = 16
 NCH = SB // ROWS
 PER = NC // 5
-FAR = 6
+FAR = 5
+LATE = 1
+SOON = NC - FAR - LATE
 CELLS = float(NB * NU * SB * SB)
 
 
@@ -176,9 +178,12 @@
     def own2(i):
         return pltpu.make_async_copy(send_of[i].at[me], mine(wide_of[i]), loc.at[i, 1])
 
-    def direct(channels):
-        part = pl.ds(0, channels)
-        return remote(l_hbm.at[part], prev_ref.at[part], zs.at[0], zr.at[0], section(1))
+    def direct(channels, start=0, i=0):
+        part = pl.ds(start, channels)
+        return remote(l_hbm.at[part], prev_ref.at[part], zs.at[i], zr.at[i], section(1))
+
+    def late():
+        return direct(LATE, SOON, 4)
 
     far = pl.ds(NC - FAR, FAR)
     flag_copy = remote(flags, flag_ref, ks.at[3], kr.at[3], section(1))
@@ -231,7 +236,7 @@
 
     @pl.when(odd)
     def _():
-        direct(NC - FAR).start()
+        direct(SOON).start()
         hop(0).start()
 
     @pl.when(jnp.logical_not(odd))
@@ -429,6 +434,12 @@
 
         if c:
             onward(c - 1).start()
+        if c == 1:
+
+            @pl.when(odd)
+            def _():
+                late().start()
+
 
     onward(2).start()
 
@@ -463,7 +474,8 @@
 
     @pl.when(odd)
     def _():
-        direct(NC - FAR).wait_send()
+        direct(SOON).wait_send()
+        late().wait_send()
         for i in range(3):
             hop(i).wait_send()
         direct(NC).wait_recv()
@@ -471,7 +483,8 @@
     @pl.when(jnp.logical_not(odd))
     def _():
         direct(NC).wait_send()
-        direct(NC - FAR).wait_recv()
+        direct(SOON).wait_recv()
+        late().wait_recv()
         hop(2).wait_recv()
 
     onward(0).wait_send()
@@ -513,7 +526,7 @@
             f32(*slots), f32(NB, *slots), f32(*slots), f32(NB, *slots), f32(*tile), f32(NB, *tile),
             f32(*slots), f32(*slots), f32(*slots), f32(*slots), f32(NB, *slots), f32(*slots),
             dma(NC), dma(NC), dma(2, 2), dma(2, 2), dma(2, NB), dma(2, NB), dma(2, NB), dma(2, NB),
-            dma(3, NB), dma(3, NB), dma(2, 2), dma(4), dma(4), dma(4), dma(4), dma(2), dma(2), dma(2),
+            dma(3, NB), dma(3, NB), dma(2, 2), dma(5), dma(5), dma(4), dma(4), dma(2), dma(2), dma(2),
         ],
         compiler_params=pltpu.CompilerParams(collective_id=0, has_side_effects=True),
         name="davidson",
@@ -586,20 +599,24 @@
                 for k in range(PER):
                     out[c + 5 * k, t] = new[:, k * SB : (k + 1) * SB]
 
-        @pl.loop(0, NU)
-        def _(t):
-            fetch_kept(t).wait()
-            fetch(prev_hbm, t).wait()
-            one(t)
-
-            @pl.when(t > 0)
+        @pl.loop(0, NU, step=2)
+        def _(t0):
+            for i in range(2):
+                fetch_kept(t0 + i).wait()
+                fetch(prev_hbm, t0 + i).wait()
+            for i in range(2):
+                one(t0 + i)
+
+            @pl.when(t0 > 0)
             def _():
-                write(out, t - 1).start()
+                for i in range(2):
+                    write(out, t0 + i - 2).start()
 
         for take, give in zip(takes, gives):
             take.wait()
             give.start()
-        write(out, NU - 1).start()
+        for i in range(2):
+            write(out, NU - 2 + i).start()
 
         @pl.loop(0, NU)
         def _(t):

time: 107 us -> 104 us (0.972); the launches traced: 106 us -> 102 us
  Pallas kernels: 105 us -> 101 us
    pallas_call x1, Pallas kernels: 93.5 us -> 90.2 us  [main_call(): pl.pallas_call(functools.partial(main_kernel, nsec), out_shape=[jax.Shape...]
    pallas_call x1, Pallas kernels: 11.8 us -> 10.7 us  [update(): pl.pallas_call(update_kernel, in_specs=[SMEM_SPEC, SMEM_SPEC] + [ANY_SPEC...]
where the time goes in v6:
time: 104 us; the launch traced here: 102 us
  Pallas kernels  101 us (97%)
    pallas_call x1, Pallas kernels, main_call(): pl.pallas_call(functools.partial(main_kernel, nsec), out_shape=[jax.Shape...  90.2 us
    pallas_call x1, Pallas kernels, update(): pl.pallas_call(update_kernel, in_specs=[SMEM_SPEC, SMEM_SPEC] + [ANY_SPEC...  10.7 us

profile of v6, /device:TPU:64, one launch (start us, length us, event | category | flops | bytes accessed | tf_op | source)
XLA Modules:
  0.0 101.5 jit_solution(6091146607097024708)
XLA Ops:
  0.6 90.2 %davidson.1 = (bf16[20,12,128,128]{3,2,1,0:T(8,128)(2,1)}, bf16[5,12,128,128]{3,2,1,0:T(8,128)(2,1)}, bf16[5,12,128,128]{3,2,1,0:T(8,128)(2,1)}, bf16[5,12,128,1...) custom-call(s32[1,12]{1,0:T(1,128)} %off_ref.1, ...), custom_call_target="tpu_custom_call" | custom-call | tf_op jit(solution)/shard_map/davidson/pallas_call | solution.py:507
  90.8 10.7 %update.1 = (bf16[20,12,128,128]{3,2,1,0:T(8,128)(2,1)}, bf16[12,128,128]{2,1,0:T(8,128)(2,1)}, bf16[12,128,128]{2,1,0:T(8,128)(2,1)}, f32[1]{0:T(128)}) custom-call(f32[16,128]{1,0:T(8,128)} %get-tuple-element.14.flag_ref, f32[8,128]{1,0:T(8,128)} %get-tuple-element.15.coef_ref, bf16[20,12,128,128]{3,2,1,0:T(8,128)(2,1)} %bitcast.8, ...), custom_call_target="tpu_custom_call" | custom-call | tf_op jit(solution)/shard_map/update/pallas_call | solution.py:631

commit v7 on v5

--- a/solution.py
+++ b/solution.py
@@ -21,7 +21,7 @@
 ROWS = 16
 NCH = SB // ROWS
 PER = NC // 5
-FAR = 6
+FAR = 5
 CELLS = float(NB * NU * SB * SB)
 
 
@@ -412,23 +412,29 @@
     def forward(j):
         return remote(kept_ref.at[0], kept_ref.at[3 + j], fs.at[j], fr.at[j], peer((1, NB - 1)[j]))
 
+    def keep(c, t):
+        if c == 0:
+            x = (v_coef * own_v(t).astype(F32) + ycoef * v1[t].astype(F32)).astype(BF16)
+            st[t] = x
+            on = lane < ranks[pl.ds(t, 1), :]
+        else:
+            x = v_coef * source(0, c, t).astype(F32) + ycoef * vs[c - 1, t].astype(F32)
+            rank = ranks_all[source_device(off_ref, t, c), pl.ds(source_slot(t, c), 1), :]
+            on = (lane < rank) & exists(off_ref, t, c)
+        kept[c, t] = jnp.where(on, x.astype(F32), 0.0).astype(BF16)
+
     for c in range(3):
-
-        @pl.loop(0, NU, step=2)
+        done = 0
+        if c:
+            for t in range(2):
+                keep(c, jnp.int32(t))
+            onward(c - 1).start()
+            done = 2
+
+        @pl.loop(done, NU, step=2)
         def _(t0):
-            for t in (t0, t0 + 1):
-                if c == 0:
-                    x = (v_coef * own_v(t).astype(F32) + ycoef * v1[t].astype(F32)).astype(BF16)
-                    st[t] = x
-                    on = lane < ranks[pl.ds(t, 1), :]
-                else:
-                    x = v_coef * source(0, c, t).astype(F32) + ycoef * vs[c - 1, t].astype(F32)
-                    rank = ranks_all[source_device(off_ref, t, c), pl.ds(source_slot(t, c), 1), :]
-                    on = (lane < rank) & exists(off_ref, t, c)
-                kept[c, t] = jnp.where(on, x.astype(F32), 0.0).astype(BF16)
-
-        if c:
-            onward(c - 1).start()
+            for i in range(2):
+                keep(c, t0 + i)
 
     onward(2).start()
 
@@ -586,20 +592,24 @@
                 for k in range(PER):
                     out[c + 5 * k, t] = new[:, k * SB : (k + 1) * SB]
 
-        @pl.loop(0, NU)
-        def _(t):
-            fetch_kept(t).wait()
-            fetch(prev_hbm, t).wait()
-            one(t)
-
-            @pl.when(t > 0)
+        @pl.loop(0, NU, step=2)
+        def _(t0):
+            for i in range(2):
+                fetch_kept(t0 + i).wait()
+                fetch(prev_hbm, t0 + i).wait()
+            for i in range(2):
+                one(t0 + i)
+
+            @pl.when(t0 > 0)
             def _():
-                write(out, t - 1).start()
+                for i in range(2):
+                    write(out, t0 + i - 2).start()
 
         for take, give in zip(takes, gives):
             take.wait()
             give.start()
-        write(out, NU - 1).start()
+        for i in range(2):
+            write(out, NU - 2 + i).start()
 
         @pl.loop(0, NU)
         def _(t):

time: 107 us -> 101 us (0.944)
  Pallas kernels: 105 us -> 98.8 us
    pallas_call x1, Pallas kernels: 93.5 us -> 88.1 us  [main_call(): pl.pallas_call(functools.partial(main_kernel, nsec), out_shape=[jax.Shape...]
    pallas_call x1, Pallas kernels: 11.8 us -> 10.7 us  [update(): pl.pallas_call(update_kernel, in_specs=[SMEM_SPEC, SMEM_SPEC] + [ANY_SPEC...]
where the time goes in v7:
time: 101 us; the launch traced here: 99.4 us
  Pallas kernels  98.8 us (98%)
    pallas_call x1, Pallas kernels, main_call(): pl.pallas_call(functools.partial(main_kernel, nsec), out_shape=[jax.Shape...  88.1 us
    pallas_call x1, Pallas kernels, update(): pl.pallas_call(update_kernel, in_specs=[SMEM_SPEC, SMEM_SPEC] + [ANY_SPEC...  10.7 us

profile of v7, /device:TPU:64, one launch (start us, length us, event | category | flops | bytes accessed | tf_op | source)
XLA Modules:
  0.0 99.4 jit_solution(17382806550376091070)
XLA Ops:
  0.6 88.1 %davidson.1 = (bf16[20,12,128,128]{3,2,1,0:T(8,128)(2,1)}, bf16[5,12,128,128]{3,2,1,0:T(8,128)(2,1)}, bf16[5,12,128,128]{3,2,1,0:T(8,128)(2,1)}, bf16[5,12,128,1...) custom-call(s32[1,12]{1,0:T(1,128)} %off_ref.1, ...), custom_call_target="tpu_custom_call" | custom-call | tf_op jit(solution)/shard_map/davidson/pallas_call | solution.py:500
  88.7 10.7 %update.1 = (bf16[20,12,128,128]{3,2,1,0:T(8,128)(2,1)}, bf16[12,128,128]{2,1,0:T(8,128)(2,1)}, bf16[12,128,128]{2,1,0:T(8,128)(2,1)}, f32[1]{0:T(128)}) custom-call(f32[16,128]{1,0:T(8,128)} %get-tuple-element.14.flag_ref, f32[8,128]{1,0:T(8,128)} %get-tuple-element.15.coef_ref, bf16[20,12,128,128]{3,2,1,0:T(8,128)(2,1)} %bitcast.8, ...), custom_call_target="tpu_custom_call" | custom-call | tf_op jit(solution)/shard_map/update/pallas_call | solution.py:624

commit v8 on v7

--- a/solution.py
+++ b/solution.py
@@ -581,16 +581,18 @@
     def _():
         def one(t):
             kept = kp[0, t]
+            wide = []
             for c in range(5):
                 stack = jnp.concatenate([lp[c + 5 * k, t] for k in range(PER)], axis=0)
                 x = kp[c, t]
                 if c > 2:
                     x = jnp.where(flag_ref[t, c - 3] > 0.5, x, jnp.zeros_like(x))
                 inner = jnp.dot(stack, x, preferred_element_type=F32).astype(BF16)
-                wide = jnp.concatenate([inner[k * SB : (k + 1) * SB] for k in range(PER)], axis=1)
-                new = lax.dot_general(kept, wide, (((0,), (0,)), ((), ())), preferred_element_type=F32).astype(BF16)
-                for k in range(PER):
-                    out[c + 5 * k, t] = new[:, k * SB : (k + 1) * SB]
+                wide += [inner[k * SB : (k + 1) * SB] for k in range(PER)]
+            every = jnp.concatenate(wide, axis=1)
+            new = lax.dot_general(kept, every, (((0,), (0,)), ((), ())), preferred_element_type=F32).astype(BF16)
+            for i in range(NC):
+                out[i // PER + 5 * (i % PER), t] = new[:, i * SB : (i + 1) * SB]
 
         @pl.loop(0, NU, step=2)
         def _(t0):

time: 101 us -> 100 us (0.990)
  no operation moved by 1% of the time
where the time goes in v8:
time: 100 us; the launch traced here: 98.7 us
  Pallas kernels  98.1 us (98%)
    pallas_call x1, Pallas kernels, main_call(): pl.pallas_call(functools.partial(main_kernel, nsec), out_shape=[jax.Shape...  88.1 us
    pallas_call x1, Pallas kernels, update(): pl.pallas_call(update_kernel, in_specs=[SMEM_SPEC, SMEM_SPEC] + [ANY_SPEC...  9.96 us

profile of v8, /device:TPU:64, one launch (start us, length us, event | category | flops | bytes accessed | tf_op | source)
XLA Modules:
  0.0 98.7 jit_solution(14754029905244106743)
XLA Ops:
  0.6 88.1 %davidson.1 = (bf16[20,12,128,128]{3,2,1,0:T(8,128)(2,1)}, bf16[5,12,128,128]{3,2,1,0:T(8,128)(2,1)}, bf16[5,12,128,128]{3,2,1,0:T(8,128)(2,1)}, bf16[5,12,128,1...) custom-call(s32[1,12]{1,0:T(1,128)} %off_ref.1, ...), custom_call_target="tpu_custom_call" | custom-call | tf_op jit(solution)/shard_map/davidson/pallas_call | solution.py:500
  88.7 10.0 %update.1 = (bf16[20,12,128,128]{3,2,1,0:T(8,128)(2,1)}, bf16[12,128,128]{2,1,0:T(8,128)(2,1)}, bf16[12,128,128]{2,1,0:T(8,128)(2,1)}, f32[1]{0:T(128)}) custom-call(f32[16,128]{1,0:T(8,128)} %get-tuple-element.14.flag_ref, f32[8,128]{1,0:T(8,128)} %get-tuple-element.15.coef_ref, bf16[20,12,128,128]{3,2,1,0:T(8,128)(2,1)} %bitcast.8, ...), custom_call_target="tpu_custom_call" | custom-call | tf_op jit(solution)/shard_map/update/pallas_call | solution.py:626
